TPU v7x, 32 devices: a whole 2x2x4 slice. The times are simulated.
32 devices in a mesh: dp: 16 (over z, y, core), seq: 2 (over x).
Axes of the slice: x: 2, y: 2, z: 4, core: 2. Of those that a mesh axis runs over, the one named last changes fastest.
Arguments:
- inputs: bfloat16 [2, 2048, 1024], P(None, ('dp', 'seq')), may hold values from -6 to 6
- cotangent: bfloat16 [2, 2048, 1024], P(None, ('dp', 'seq')), may hold values from -6 to 6
- w_qkv: bfloat16 [1024, 3072], P('dp'), may hold values from -0.1875 to 0.1875
- w_out: bfloat16 [1024, 1024], P('dp'), may hold values from -0.75 to 0.75
- w_up: bfloat16 [1024, 4096], P('dp'), may hold values from -0.1875 to 0.1875
- w_down: bfloat16 [4096, 1024], P('dp'), may hold values from -0.09375 to 0.09375
- bias_q: bfloat16 [1024], P('dp'), may hold values from -3 to 3
- bias_v: bfloat16 [1024], P('dp'), may hold values from -3 to 3
- bias_out: bfloat16 [1024], P('dp'), may hold values from -3 to 3
- gain_one: bfloat16 [1024], P('dp'), may hold values from 0.5 to 1.5
- shift_one: bfloat16 [1024], P('dp'), may hold values from -3 to 3
- bias_up: bfloat16 [4096], P('dp'), may hold values from -3 to 3
- bias_down: bfloat16 [1024], P('dp'), may hold values from -3 to 3
- gain_two: bfloat16 [1024], P('dp'), may hold values from 0.5 to 1.5
- shift_two: bfloat16 [1024], P('dp'), may hold values from -3 to 3
Outputs:
- layer_out: bfloat16 [2, 2048, 1024], P(None, ('dp', 'seq'))
- input_grad: float32 [2, 2048, 1024], P(None, ('dp', 'seq'))
- grad_qkv: float32 [1024, 3072], P('dp')
- grad_out: float32 [1024, 1024], P('dp')
- grad_up: float32 [1024, 4096], P('dp')
- grad_down: float32 [4096, 1024], P('dp')
- grad_bias_q: float32 [1024], P('dp')
- grad_bias_v: float32 [1024], P('dp')
- grad_bias_out: float32 [1024], P('dp')
- grad_gain_one: float32 [1024], P('dp')
- grad_shift_one: float32 [1024], P('dp')
- grad_bias_up: float32 [4096], P('dp')
- grad_bias_down: float32 [1024], P('dp')
- grad_gain_two: float32 [1024], P('dp')
- grad_shift_two: float32 [1024], P('dp')
All inputs are finite; a program needn't handle non-finite values.
Results may differ from a plain program's by a relative error of at most 0.015.
Values may be sent and summed in bfloat16 or wider, within the bound.
No kernel may reach another device: no remote copies, remote signals or barrier semaphores. Data moves between devices by JAX's collectives and lax.ppermute only.
A program may use at most 192 MiB of HBM per device.

v0:
```python
import functools
import math

import jax
import jax.numpy as jnp
from jax import lax
from jax.experimental import pallas as pl
from jax.experimental.pallas import tpu as pltpu
from jax.sharding import PartitionSpec as P

HEAD = 64
CORES = 2
PARTS = 8
SHORT = jnp.bfloat16
WIDE = jnp.float32
LIMIT = 56 * 1024 * 1024
LINES = 16
LANES = 256


def gelu_exact(values):
    return 0.5 * values * (1.0 + lax.erf(values * (1.0 / math.sqrt(2.0))))


def gelu_slope(values):
    bell = jnp.exp(values * values * -0.5) * (1.0 / math.sqrt(2.0 * math.pi))
    return 0.5 * (1.0 + lax.erf(values * (1.0 / math.sqrt(2.0)))) + values * bell


def times(left, right):
    return jnp.dot(left, right, preferred_element_type=WIDE)


def times_back(left, right):
    return lax.dot_general(left, right, (((1,), (1,)), ((), ())), preferred_element_type=WIDE)


def inner_rows(left, right):
    return lax.dot_general(left, right, (((0,), (0,)), ((), ())), preferred_element_type=WIDE)


def column_sum(part):
    return jnp.sum(part, axis=0, keepdims=True)


def standard(features):
    centre = jnp.mean(features, axis=-1, keepdims=True)
    centred = features - centre
    spread = jnp.mean(centred * centred, axis=-1, keepdims=True)
    slope = lax.rsqrt(spread + 1e-12)
    return centred * slope, slope


def standard_back(normal, slope, grad):
    even = jnp.mean(grad, axis=-1, keepdims=True)
    along = jnp.mean(normal * grad, axis=-1, keepdims=True)
    return slope * (grad - even - normal * along)


def pick(array, index, axis):
    return lax.dynamic_index_in_dim(array, index, axis, keepdims=False)


def in_order(place, own, other, axis):
    first = place == 0
    return jnp.stack([jnp.where(first, own, other), jnp.where(first, other, own)], axis=axis)


def block(index, size):
    return pl.ds(pl.multiple_of(index * size, size), size)


def here():
    index = lax.axis_index("dp")
    return lax.div(index, CORES), lax.rem(index, CORES), lax.axis_index("seq")


def part_index(step, flip, ringed, chip, chips):
    if not ringed:
        return step
    half = chips // 2
    upper = lax.rem(chip, 2)
    level = lax.div(chip, 2)
    spot = jnp.where(upper == 0, level, chips - 1 - level)
    away = (step + 1) // 2
    sign = -1 if (step % 2 == 1) != flip else 1
    spot = lax.rem(spot + sign * away + chips, chips)
    return jnp.where(spot < half, 2 * spot, 2 * (chips - 1 - spot) + 1)


def call(body, outs, scratch=(), flops=0, moved=0):
    return pl.pallas_call(
        body,
        out_shape=[jax.ShapeDtypeStruct(shape, kind) for shape, kind in outs],
        scratch_shapes=[pltpu.VMEM(shape, kind) for shape, kind in scratch],
        compiler_params=pltpu.CompilerParams(vmem_limit_bytes=LIMIT),
        cost_estimate=pl.CostEstimate(flops=flops, bytes_accessed=moved, transcendentals=0),
    )


def pack_kernel(*refs):
    vectors, up_bias, w_qkv, w_out, mine, theirs = refs[:8], *refs[8:]
    _, core, half = here()
    depth = w_qkv.shape[0]
    width = w_out.shape[1]
    quarter = width // 4
    for out, which in ((mine, core), (theirs, 1 - core)):
        for third in range(3):
            start = third * width + (2 * half + which) * quarter
            out[:depth, third * quarter : (third + 1) * quarter] = w_qkv[
                :, pl.ds(pl.multiple_of(start, quarter), quarter)
            ]
        out[:depth, 3 * quarter :] = w_out[:, block(which, width // 2)]
        lines = [
            jnp.pad(vector[...], ((0, 0), (0, LANES - depth))).astype(WIDE) for vector in vectors
        ]
        lines.append(jnp.pad(up_bias[...].astype(WIDE), ((0, 0), (0, LANES - up_bias.shape[1]))))
        lines.append(jnp.zeros((LINES - 9, LANES), WIDE))
        out[depth:, :LANES] = jnp.concatenate(lines, axis=0).astype(SHORT)
        out[depth:, LANES:] = jnp.zeros((LINES, out.shape[1] - LANES), SHORT)


def heads_of(qkv, rows, head, quarter):
    return [
        qkv[rows, third * quarter + head * HEAD : third * quarter + (head + 1) * HEAD]
        for third in range(3)
    ]


def softmax(queries, keys, scale):
    scores = times_back(queries, keys) * scale
    expo = jnp.exp(scores - jnp.max(scores, axis=-1, keepdims=True))
    return expo / jnp.sum(expo, axis=-1, keepdims=True)


def fill_group(group, pieces, micro):
    rows = pieces[0].shape[0] // micro
    for place in range(4 * micro):
        far, item, side = place // (2 * micro), place // 2 % micro, place % 2
        group[place * rows : (place + 1) * rows, :] = pieces[2 * far + side][
            item * rows : (item + 1) * rows, :
        ]


def attention_kernel(micro, where, *refs):
    pieces, chunks, rest = refs[:4], refs[4:12], refs[12:]
    tokens, full, qkv, keep, send, vectors, up_bias, out_half, wide = rest
    chip, core, half = here()
    quarter = keep.shape[1]
    scale = 1.0 / math.sqrt(HEAD)
    fill_group(tokens, pieces, micro)
    for step in range(PARTS):
        spot = block(where(step, chip), 128)
        chunk = chunks[step]
        full[spot, :] = chunk[:128, : 3 * quarter]
        out_half[spot, :] = chunk[:128, 3 * quarter :]
        lines = jnp.concatenate([chunk[128:, :64], chunk[128:, LANES : LANES + 64]], axis=1)
        vectors[:, spot] = lines.astype(WIDE)
        lines = chunk[128:, block(core * (LANES // 128) + half, 128)]
        up_bias[:, spot] = lines.astype(WIDE)[8:9, :]
    wide[...] = times(tokens[...], full[...])
    spot = block(2 * half + core, quarter)
    qkv[:, :quarter] = (wide[:, :quarter] + vectors[0:1, spot]).astype(SHORT)
    qkv[:, quarter : 2 * quarter] = wide[:, quarter : 2 * quarter].astype(SHORT)
    qkv[:, 2 * quarter :] = (wide[:, 2 * quarter :] + vectors[1:2, spot]).astype(SHORT)
    length = tokens.shape[0] // (2 * micro)
    rows = length // 2
    for item in range(2 * micro):
        for pair in range(quarter // 128):
            both = []
            for head in (2 * pair, 2 * pair + 1):
                queries, keys, values = heads_of(
                    qkv, slice(item * length, (item + 1) * length), head, quarter
                )
                probs = softmax(queries, keys, scale).astype(SHORT)
                both.append(times(probs, values))
            both = jnp.concatenate(both, axis=1).astype(SHORT)
            spot = slice(pair * 128, (pair + 1) * 128)
            keep[item * rows : (item + 1) * rows, spot] = both[:rows]
            send[item * rows : (item + 1) * rows, spot] = both[rows:]


def first_kernel(
    inputs, keep, from_seq, from_core, mine, other, vectors, resid, first, low, context
):
    _, core, half = here()
    rows, width = inputs.shape
    quarter = width // 4
    flip_core, flip_half = 1 - core, 1 - half
    context[:, block(2 * half + core, quarter)] = keep[:rows, :]
    context[:, block(2 * flip_half + core, quarter)] = from_seq[:rows, :]
    context[:, block(2 * half + flip_core, quarter)] = from_core[:, :quarter]
    context[:, block(2 * flip_half + flip_core, quarter)] = from_core[:, quarter:]
    whole = context[...]
    resid[:, block(core, width // 2)] = times(whole, mine[...])
    resid[:, block(flip_core, width // 2)] = times(whole, other[...])
    features = inputs[...].astype(WIDE) + (resid[...] + vectors[2:3, :])
    resid[...] = features
    normal, _ = standard(features)
    features = normal * vectors[3:4, :] + vectors[4:5, :]
    first[...] = features
    low[...] = features.astype(SHORT)


def split_rows(value, start, micro, rows, keep, send):
    for place in range(value.shape[0] // rows):
        far, item, side = (
            (start + place * rows) // rows // (2 * micro),
            (start + place * rows) // rows // 2 % micro,
            (start + place * rows) // rows % 2,
        )
        part = value[place * rows : (place + 1) * rows, :]
        if far:
            send[side, item * rows : (item + 1) * rows, :] = part.astype(SHORT)
        else:
            keep[side, item * rows : (item + 1) * rows, :] = part


def forward_kernel(micro, where, *refs):
    pieces, chunks, up_bias, rest = refs[:4], refs[4:12], refs[12], refs[13:]
    group, full_up, full_down, pre_act, act, keep, send = rest
    chip, _, _ = here()
    fill_group(group, pieces, micro)
    for step in range(PARTS):
        spot = block(where(step, chip), 128)
        full_up[spot, :] = chunks[step][:128, :]
        full_down[spot, :] = chunks[step][128:, :]
    rows = pieces[0].shape[0] // micro
    tall = group.shape[0] // 2
    for side in range(2):
        spot = slice(side * tall, (side + 1) * tall)
        pre = times(group[spot, :], full_up[...]) + up_bias[...]
        pre_act[spot, :] = pre
        act[spot, :] = gelu_exact(pre).astype(SHORT)
        out = times(act[spot, :], full_down[...])
        split_rows(out, side * tall, micro, rows, keep, send)


def second_kernel(
    first, keep, from_core, from_seq, vectors, cotangent, out, grad, low, sums
):
    mlp = keep[0] + from_core[0].astype(WIDE) + from_seq[...].astype(WIDE)
    normal, slope = standard(first[...] + (mlp + vectors[5:6, :]))
    out[...] = (normal * vectors[6:7, :] + vectors[7:8, :]).astype(SHORT)
    incoming = cotangent[...].astype(WIDE)
    resid = standard_back(normal, slope, incoming * vectors[6:7, :])
    grad[...] = resid
    short = resid.astype(SHORT)
    low[...] = short
    sums[...] = jnp.zeros_like(sums)
    sums[0:1, :] = column_sum(short.astype(WIDE))
    sums[1:2, :] = column_sum(incoming * normal)
    sums[2:3, :] = column_sum(incoming)


def backward_kernel(micro, where, *refs):
    pieces, rest = refs[:4], refs[4:]
    group, full_up, full_down, pre_act, act, chunks, keep, send, sums, grad, pre = rest
    chip, _, _ = here()
    fill_group(grad, pieces, micro)
    rows = pieces[0].shape[0] // micro
    tall = grad.shape[0] // 2
    total = None
    for side in range(2):
        spot = slice(side * tall, (side + 1) * tall)
        slope = gelu_slope(pre_act[spot, :])
        part = (times_back(grad[spot, :], full_down[...]) * slope).astype(SHORT)
        pre[spot, :] = part
        part = column_sum(part.astype(WIDE))
        total = part if total is None else total + part
    sums[...] = total
    for step in range(PARTS):
        spot = block(where(step, chip), 128)
        chunks[step, 128:, :] = inner_rows(act[:, spot], grad[...]).astype(SHORT)
        chunks[step, :128, :] = inner_rows(group[:, spot], pre[...]).astype(SHORT)
    for side in range(2):
        spot = slice(side * tall, (side + 1) * tall)
        out = times_back(pre[spot, :], full_up[...])
        split_rows(out, side * tall, micro, rows, keep, send)


def first_back_kernel(
    resid,
    grad_two,
    keep,
    from_core,
    from_seq,
    vectors,
    context,
    mine,
    other,
    grad,
    out_keep,
    out_send,
    ctx_keep,
    ctx_send,
    sums,
):
    _, core, half = here()
    width = resid.shape[1]
    quarter = width // 4
    incoming = grad_two[...] + (keep[0] + from_core[0].astype(WIDE) + from_seq[...].astype(WIDE))
    normal, slope = standard(resid[...])
    value = standard_back(normal, slope, incoming * vectors[3:4, :])
    grad[...] = value
    short = value.astype(SHORT)
    sums[...] = jnp.zeros_like(sums)
    sums[0:1, :] = column_sum(short.astype(WIDE))
    sums[1:2, :] = column_sum(incoming * normal)
    sums[2:3, :] = column_sum(incoming)
    left, right = short[:, : width // 2], short[:, width // 2 :]
    own = jnp.where(core == 0, left, right)
    away = jnp.where(core == 0, right, left)
    out_keep[...] = inner_rows(context[...], own)
    out_send[...] = inner_rows(context[...], away).astype(SHORT)
    for target, which in ((ctx_keep, core), (ctx_send, 1 - core)):
        for side, which_half in enumerate((half, 1 - half)):
            spot = block(2 * which_half + which, quarter)
            value = times_back(own, mine[spot, :]) + times_back(away, other[spot, :])
            target[:, side * quarter : (side + 1) * quarter] = value.astype(SHORT)


def attention_back_kernel(micro, where, *refs):
    qkv, ctx_keep, ctx_core, ctx_seq, tokens, full, out_keep, out_core = refs[:8]
    sums_two, sums_one, up_sums, chunks, keep, send, grad, vectors = refs[8:]
    chip, core, half = here()
    quarter = qkv.shape[1] // 3
    length = qkv.shape[0] // (2 * micro)
    rows = length // 2
    scale = 1.0 / math.sqrt(HEAD)
    for item in range(2 * micro):
        spot = slice(item * length, (item + 1) * length)
        near = ctx_keep if item < micro else ctx_core
        inner = slice(item % micro * rows, (item % micro + 1) * rows)
        outer = slice(item * rows, (item + 1) * rows)
        for pair in range(quarter // 128):
            lanes = slice(pair * 128, (pair + 1) * 128)
            incoming = jnp.concatenate([near[inner, lanes], ctx_seq[outer, lanes]], axis=0)
            results = [[], [], []]
            for side in range(2):
                queries, keys, values = heads_of(qkv, spot, 2 * pair + side, quarter)
                probs = softmax(queries, keys, scale)
                own = incoming[:, side * HEAD : (side + 1) * HEAD]
                grad_probs = times_back(own, values)
                along = jnp.sum(probs * grad_probs, axis=-1, keepdims=True)
                grad_scores = (probs * (grad_probs - along)).astype(SHORT)
                results[0].append(times(grad_scores, keys) * scale)
                results[1].append(inner_rows(grad_scores, queries) * scale)
                results[2].append(inner_rows(probs.astype(SHORT), own))
            for third in range(3):
                start = third * quarter + pair * 128
                grad[spot, start : start + 128] = jnp.concatenate(results[third], axis=1).astype(
                    SHORT
                )
    line = column_sum(grad[...].astype(WIDE))
    vectors[...] = jnp.zeros_like(vectors)
    vectors[0:1, block(2 * half + core, quarter)] = line[:, :quarter]
    vectors[1:2, block(2 * half + core, quarter)] = line[:, 2 * quarter :]
    vectors[2:5, :] = sums_one[0:3, :]
    vectors[5:8, :] = sums_two[0:3, :]
    vectors[8:9, :] = up_sums[...]
    for step in range(PARTS):
        spot = block(where(step, chip), 128)
        chunks[step, :128, : 3 * quarter] = inner_rows(tokens[:, spot], grad[...]).astype(SHORT)
        chunks[step, :128, 3 * quarter :] = (
            out_keep[spot, :] + out_core[spot, :].astype(WIDE)
        ).astype(SHORT)
        lines = vectors[:, spot].astype(SHORT)
        chunks[step, 128:, :] = jnp.zeros((LINES, chunks.shape[2]), SHORT)
        chunks[step, 128:, :64] = lines[:, :64]
        chunks[step, 128:, LANES : LANES + 64] = lines[:, 64:]
        chunks[step, 128:, 2 * LANES : 2 * LANES + 128] = lines
    tall = tokens.shape[0] // 2
    for side in range(2):
        out = times_back(grad[side * tall : (side + 1) * tall, :], full[...])
        split_rows(out, side * tall, micro, rows, keep, send)


def build(mesh):
    devices = mesh.shape["dp"]
    chips = devices // CORES
    ringed = chips == PARTS
    half_ring = chips // 2
    ring = [2 * i for i in range(half_ring)] + [2 * i + 1 for i in reversed(range(half_ring))]
    same_core = [list(range(core, devices, CORES)) for core in range(CORES)]
    core_pairs = [(i, i ^ 1) for i in range(devices)]

    def hop(step):
        return [
            (ring[i] * CORES + core, ring[(i + step) % chips] * CORES + core)
            for i in range(chips)
            for core in range(CORES)
        ]

    onward, backward = hop(1), hop(-1)

    def swap_core(array):
        return lax.ppermute(array, "dp", core_pairs)

    def swap_seq(array):
        return lax.ppermute(array, "seq", [(0, 1), (1, 0)])

    def gather_ring(chunk, flip):
        far, near = (backward, onward) if flip else (onward, backward)
        got = [chunk]
        one = two = chunk
        for step in range(1, chips // 2 + 1):
            one = lax.ppermute(one, "dp", far)
            got.append(one)
            if step < chips // 2:
                two = lax.ppermute(two, "dp", near)
                got.append(two)
        return got

    def sum_ring(parts, flip):
        far, near = (onward, backward) if flip else (backward, onward)

        def run(perm, steps):
            moving = parts[steps[0]]
            for step in steps[1:]:
                moving = lax.ppermute(moving, "dp", perm)
                moving = (moving.astype(WIDE) + parts[step].astype(WIDE)).astype(SHORT)
            return lax.ppermute(moving, "dp", perm).astype(WIDE)

        long = list(range(chips - 1, 0, -2))
        short = list(range(chips - 2, 0, -2))
        return run(far, long) + run(near, short) + parts[0].astype(WIDE)

    def where(flip, step, chip):
        return part_index(step, flip, ringed, chip, chips)

    where_one = functools.partial(where, False)
    where_two = functools.partial(where, True)

    def per_device(
        inputs,
        cotangent,
        w_qkv,
        w_out,
        w_up,
        w_down,
        bias_q,
        bias_v,
        bias_out,
        gain_one,
        shift_one,
        bias_up,
        bias_down,
        gain_two,
        shift_two,
    ):
        index = lax.axis_index("dp")
        core = index % CORES
        half = lax.axis_index("seq")
        micro, rows, width = inputs.shape
        own_rows = micro * rows
        group = 4 * own_rows
        depth = w_qkv.shape[0]
        units = w_down.shape[0]
        tall = w_up.shape[1]
        quarter = width // 4
        side = 3 * quarter + width // 2
        several = chips // PARTS

        def share(own):
            from_seq = swap_seq(own)
            return own, from_seq, swap_core(own), swap_core(from_seq)

        def finish_sum(keep, from_core):
            moving = (keep[1] + from_core[1].astype(WIDE)).astype(SHORT)
            return swap_seq(moving)

        vectors = (
            bias_q,
            bias_v,
            bias_out,
            gain_one,
            shift_one,
            bias_down,
            gain_two,
            shift_two,
            bias_up,
        )
        mine, theirs = call(pack_kernel, [((depth + LINES, side), SHORT)] * 2, moved=10**6)(
            *[vector.reshape(1, -1) for vector in vectors], w_qkv, w_out
        )
        theirs = swap_core(theirs)
        square = in_order(core, mine[:depth], theirs[:depth], 0).reshape(2 * depth, side)
        lines = in_order(core, mine[depth:, :LANES], theirs[depth:, :LANES], 1)
        lines = jnp.pad(lines.reshape(LINES, 2 * LANES), ((0, 0), (0, side - 2 * LANES)))
        chunk_one = jnp.concatenate([square, lines], axis=0)

        by_unit = w_up.reshape(depth, chips, 2, 2, units // 2)
        by_unit = pick(by_unit, half, 3)
        mine = pick(by_unit, core, 2).reshape(depth, tall // 4)
        theirs = pick(by_unit, 1 - core, 2).reshape(depth, tall // 4)
        both = in_order(core, mine, swap_core(theirs), 0).reshape(2 * depth, tall // 4)
        own_down = pick(w_down.reshape(2, units // 2, width), half, 0)
        chunk_two = jnp.concatenate([both, own_down], axis=0)

        if ringed:
            chunks_one = gather_ring(chunk_one, False)
            chunk_two, _ = lax.optimization_barrier((chunk_two, chunks_one[5]))
            chunks_two = gather_ring(chunk_two, True)
        else:
            whole = lax.all_gather(chunk_one, "dp", axis_index_groups=same_core)
            square = whole[:, : 2 * depth].reshape(PARTS, 128, side)
            lines = whole[:, 2 * depth :, : 2 * LANES].reshape(chips, LINES, 2, LANES)
            slim = lines[:, :8, :, :depth].reshape(PARTS, several, 8, 2 * depth)
            slim = slim.transpose(0, 2, 1, 3).reshape(PARTS, 8, 2, 64)
            slim = jnp.pad(slim, ((0, 0), (0, 0), (0, 0), (0, LANES - 64)))
            slim = slim.reshape(PARTS, 8, 2 * LANES)
            bias = pick(lines[:, 8, :, :units], core, 1).reshape(chips, 2, units // 2)
            bias = pick(bias, half, 1).reshape(PARTS, 1, 128)
            lines = jnp.concatenate([slim, jnp.tile(bias, (1, 1, 2 * LANES // 128))], axis=1)
            lines = jnp.pad(lines, ((0, 0), (0, LINES - 9), (0, side - 2 * LANES)))
            whole = jnp.concatenate([square, lines], axis=1)
            chunks_one = [whole[step] for step in range(PARTS)]
            whole = lax.all_gather(chunk_two, "dp", axis_index_groups=same_core)
            whole = jnp.concatenate(
                [
                    whole[:, : 2 * depth].reshape(PARTS, 128, width),
                    whole[:, 2 * depth :].reshape(PARTS, 128, width),
                ],
                axis=1,
            )
            chunks_two = [whole[step] for step in range(PARTS)]

        flat = inputs.reshape(own_rows, width)
        tokens, full_qkv, qkv, ctx_keep, ctx_send, table, up_bias, out_mine = call(
            functools.partial(attention_kernel, micro, where_one),
            [
                ((group, width), SHORT),
                ((width, 3 * quarter), SHORT),
                ((group, 3 * quarter), SHORT),
                ((group // 2, quarter), SHORT),
                ((group // 2, quarter), SHORT),
                ((LINES, width), WIDE),
                ((1, tall // 4), WIDE),
                ((width, width // 2), SHORT),
            ],
            [((group, 3 * quarter), WIDE)],
            flops=2 * group * width * width,
            moved=8 * 10**6,
        )(*share(flat), *chunks_one)
        out_other = swap_core(out_mine)
        ctx_seq = swap_seq(ctx_send)
        ctx_core = swap_core(
            jnp.concatenate([ctx_keep[own_rows:], ctx_seq[own_rows:]], axis=1)
        )
        resid, first, first_low, context = call(
            first_kernel,
            [
                ((own_rows, width), WIDE),
                ((own_rows, width), WIDE),
                ((own_rows, width), SHORT),
                ((own_rows, width), SHORT),
            ],
            flops=2 * own_rows * width * width,
            moved=4 * 10**6,
        )(flat, ctx_keep, ctx_seq, ctx_core, out_mine, out_other, table)

        split_out = [((2, own_rows, width), WIDE), ((2, own_rows, width), SHORT)]
        first_group, full_up, full_down, pre_act, act, keep, send = call(
            functools.partial(forward_kernel, micro, where_two),
            [
                ((group, width), SHORT),
                ((width, tall // 4), SHORT),
                ((tall // 4, width), SHORT),
                ((group, tall // 4), WIDE),
                ((group, tall // 4), SHORT),
            ]
            + split_out,
            flops=group * width * tall,
            moved=16 * 10**6,
        )(*share(first_low), *chunks_two, up_bias)
        from_core = swap_core(send)
        from_seq = finish_sum(keep, from_core)
        layer_out, grad_two, mlp_low, sums_two = call(
            second_kernel,
            [
                ((own_rows, width), SHORT),
                ((own_rows, width), WIDE),
                ((own_rows, width), SHORT),
                ((8, width), WIDE),
            ],
            moved=3 * 10**6,
        )(first, keep, from_core, from_seq, table, cotangent.reshape(own_rows, width))

        grads_two, keep, send, up_sums = call(
            functools.partial(backward_kernel, micro, where_two),
            [((PARTS, 256, width), SHORT)] + split_out + [((1, tall // 4), WIDE)],
            [((group, width), SHORT), ((group, tall // 4), SHORT)],
            flops=2 * group * width * tall,
            moved=16 * 10**6,
        )(*share(mlp_low), first_group, full_up, full_down, pre_act, act)
        from_core = swap_core(send)
        from_seq = finish_sum(keep, from_core)
        grad_one, out_keep, out_send, grad_keep, grad_send, sums_one = call(
            first_back_kernel,
            [
                ((own_rows, width), WIDE),
                ((width, width // 2), WIDE),
                ((width, width // 2), SHORT),
                ((own_rows, width // 2), SHORT),
                ((own_rows, width // 2), SHORT),
                ((8, width), WIDE),
            ],
            flops=4 * own_rows * width * width,
            moved=8 * 10**6,
        )(resid, grad_two, keep, from_core, from_seq, table, context, out_mine, out_other)
        grad_core = swap_core(grad_send)
        grad_seq = swap_seq(jnp.concatenate([grad_keep[:, quarter:], grad_core[:, quarter:]]))
        out_core = swap_core(out_send)
        grads_one, keep, send = call(
            functools.partial(attention_back_kernel, micro, where_one),
            [((PARTS, 128 + LINES, side), SHORT)] + split_out,
            [((group, 3 * quarter), SHORT), ((LINES, width), WIDE)],
            flops=3 * group * width * width,
            moved=12 * 10**6,
        )(
            qkv,
            grad_keep,
            grad_core,
            grad_seq,
            tokens,
            full_qkv,
            out_keep,
            out_core,
            sums_two,
            sums_one,
            up_sums,
        )
        from_core = swap_core(send)
        from_seq = finish_sum(keep, from_core)
        input_grad = grad_one + (keep[0] + from_core[0].astype(WIDE) + from_seq.astype(WIDE))

        if ringed:
            share_two = sum_ring(grads_two, True)
            share_one = sum_ring(grads_one, False)
        else:
            whole = jnp.concatenate(
                [
                    grads_two[:, :128].reshape(chips, 2 * depth, width),
                    grads_two[:, 128:].reshape(chips, units // 2, width),
                ],
                axis=1,
            )
            share_two = lax.psum_scatter(whole, "dp", axis_index_groups=same_core).astype(WIDE)
            square = grads_one[:, :128].reshape(chips, 2 * depth, side)
            slim = grads_one[:, 128 : 128 + 8, : 2 * LANES].reshape(PARTS, 8, 2, LANES)[..., :64]
            slim = slim.reshape(PARTS, 8, several, 2 * depth).transpose(0, 2, 1, 3)
            slim = slim.reshape(chips, 8, 2, depth)
            slim = jnp.pad(slim, ((0, 0), (0, LINES - 8), (0, 0), (0, LANES - depth)))
            bias = grads_one[:, 128 + 8, 2 * LANES : 2 * LANES + 128]
            bias = bias.reshape(chips, 1, units // 2)
            bias = jnp.pad(
                bias, ((0, 0), (8, LINES - 9), (0, side - 2 * LANES - units // 2))
            )
            lines = jnp.concatenate([slim.reshape(chips, LINES, 2 * LANES), bias], axis=2)
            whole = jnp.concatenate([square, lines], axis=1)
            share_one = lax.psum_scatter(whole, "dp", axis_index_groups=same_core).astype(WIDE)

        split = share_two[: 2 * depth].reshape(2, depth, width).astype(SHORT)
        own, other = pick(split, core, 0), swap_core(pick(split, 1 - core, 0))
        own_down = share_two[2 * depth :].astype(SHORT)
        moved = swap_seq(jnp.concatenate([own, other, own_down], axis=0))
        by_chip = (depth, chips, units // 2)
        near = in_order(core, own.reshape(by_chip), other.reshape(by_chip), 2)
        away = in_order(
            core, moved[:depth].reshape(by_chip), moved[depth : 2 * depth].reshape(by_chip), 2
        )
        final_up = in_order(half, near, away, 3).reshape(depth, tall).astype(WIDE)
        final_down = in_order(half, own_down, moved[2 * depth :], 0)
        final_down = final_down.reshape(units, width).astype(WIDE)

        split = share_one[: 2 * depth].reshape(2, depth, side).astype(SHORT)
        lines = share_one[2 * depth :, : 2 * LANES].reshape(LINES, 2, LANES)
        packet = jnp.pad(pick(lines, 1 - core, 1).astype(SHORT), ((0, 0), (0, side - LANES)))
        other = swap_core(jnp.concatenate([pick(split, 1 - core, 0), packet], axis=0))
        own = pick(split, core, 0)
        line = pick(lines, core, 1) + other[depth:, :LANES].astype(WIDE)
        bias = share_one[2 * depth + 8, 2 * LANES : 2 * LANES + units // 2]
        packet = jnp.concatenate(
            [line.astype(SHORT), share_one[2 * depth :, 2 * LANES :].astype(SHORT)], axis=1
        )
        packet = jnp.pad(packet, ((0, 0), (0, LANES)))
        moved = swap_seq(jnp.concatenate([own, other[:depth], packet], axis=0))
        by_third = (depth, 3, quarter)
        near = in_order(
            core,
            own[:, : 3 * quarter].reshape(by_third),
            other[:depth, : 3 * quarter].reshape(by_third),
            2,
        )
        away = in_order(
            core,
            moved[:depth, : 3 * quarter].reshape(by_third),
            moved[depth : 2 * depth, : 3 * quarter].reshape(by_third),
            2,
        )
        final_qkv = in_order(half, near, away, 2).reshape(depth, 3 * width).astype(WIDE)
        near = own[:, 3 * quarter :].astype(WIDE) + moved[:depth, 3 * quarter :].astype(WIDE)
        away = other[:depth, 3 * quarter :].astype(WIDE) + moved[
            depth : 2 * depth, 3 * quarter :
        ].astype(WIDE)
        final_out = in_order(core, near, away, 1).reshape(depth, width)
        line = line + moved[2 * depth :, :LANES].astype(WIDE)
        finals = [line[i, :depth] for i in range(8)]
        from_seq = moved[2 * depth + 8, LANES : LANES + units // 2].astype(WIDE)
        final_bias = in_order(half, bias, from_seq, 0).reshape(-1)

        return (
            layer_out.reshape(inputs.shape),
            input_grad.reshape(inputs.shape),
            final_qkv,
            final_out,
            final_up,
            final_down,
            finals[0],
            finals[1],
            finals[2],
            finals[3],
            finals[4],
            final_bias,
            finals[5],
            finals[6],
            finals[7],
        )

    return per_device


def solution(mesh):
    token = P(None, ("dp", "seq"), None)
    matrix = P("dp", None)
    vector = P("dp")
    placed = (token, token) + (matrix,) * 4 + (vector,) * 9
    return jax.shard_map(
        build(mesh), mesh=mesh, in_specs=placed, out_specs=placed, check_vma=False
    )
```

profile of v0, /device:TPU:0, one launch (start us, length us, event | category | flops | bytes accessed | tf_op | source)
XLA Modules:
  0.0 283.6 jit_solution(9069441774863462851)
XLA Ops:
  10.4 8.8 %collective-permute-done.4.refs_5_ = bf16[144,1280]{1,0:T(8,128)(2,1)S(1)} collective-permute-done((bf16[144,1280]{1,0:T(8,128)(2,1)S(1)}, bf16[144,1280]{1,0:T(8,128)(2,1)S(1)}, u32[]{:S(2)}, u32[]{:S(2)}) %collective-permute-start.4) | collective-permute-done | bytes 368672 | tf_op jit(solution)/shard_map/ppermute | solution.py:408
  25.2 4.2 %collective-permute-done.6.refs_7_ = bf16[144,1280]{1,0:T(8,128)(2,1)S(1)} collective-permute-done((bf16[144,1280]{1,0:T(8,128)(2,1)S(1)}, bf16[144,1280]{1,0:T(8,128)(2,1)S(1)}, u32[]{:S(2)}, u32[]{:S(2)}) %collective-permute-start.6) | collective-permute-done | bytes 368672 | tf_op jit(solution)/shard_map/ppermute | solution.py:408
  31.0 7.6 %collective-permute-done.8.refs_9_ = bf16[144,1280]{1,0:T(8,128)(2,1)S(1)} collective-permute-done((bf16[144,1280]{1,0:T(8,128)(2,1)S(1)}, bf16[144,1280]{1,0:T(8,128)(2,1)S(1)}, u32[]{:S(2)}, u32[]{:S(2)}) %collective-permute-start.8) | collective-permute-done | bytes 368672 | tf_op jit(solution)/shard_map/ppermute | solution.py:408
  44.2 13.9 %collective-permute-done.9.refs_10_ = bf16[144,1280]{1,0:T(8,128)(2,1)S(1)} collective-permute-done((bf16[144,1280]{1,0:T(8,128)(2,1)S(1)}, bf16[144,1280]{1,0:T(8,128)(2,1)S(1)}, u32[]{:S(2)}, u32[]{:S(2)}) %collective-permute-start.9) | collective-permute-done | bytes 368672 | tf_op jit(solution)/shard_map/ppermute | solution.py:411
  59.7 9.4 %shard_map.263 = (bf16[512,1024]{1,0:T(8,128)(2,1)}, bf16[1024,768]{1,0:T(8,128)(2,1)}, bf16[512,768]{1,0:T(8,128)(2,1)}, bf16[256,256]{1,0:T(8,128)(2,1)}, bf16...) custom-call(bf16[128,1024]{1,0:T(8,128)(2,1)} %bitcast.181, ...), custom_call_target="tpu_custom_call" | custom-call | flops 1073741824 | bytes 8000000 | tf_op jit(solution)/shard_map/pallas_call | solution.py:530
  71.3 12.2 %collective-permute-done.20.refs_7_ = bf16[256,1024]{1,0:T(8,128)(2,1)S(1)} collective-permute-done((bf16[256,1024]{1,0:T(8,128)(2,1)S(1)}, bf16[256,1024]{1,0:T(8,128)(2,1)S(1)}, u32[]{:S(2)}, u32[]{:S(2)}) %collective-permute-start.20) | collective-permute-done | bytes 524320 | tf_op jit(solution)/shard_map/ppermute | solution.py:408
  91.9 3.5 %shard_map.264 = (f32[128,1024]{1,0:T(8,128)}, f32[128,1024]{1,0:T(8,128)}, bf16[128,1024]{1,0:T(8,128)(2,1)}, bf16[128,1024]{1,0:T(8,128)(2,1)}) custom-call(bf16[128,1024]{1,0:T(8,128)(2,1)} %bitcast.182, bf16[256,256]{1,0:T(8,128)(2,1)} %get-tuple-element.56.keep, bf16[256,256]{1,0:T(8,128)(2,1)} %copy-done.24, bf16[128,512]{1,0:T(8,128)(2,1)} %copy-done.31, ...), custom_call_target="tpu_custom_call" | custom-call | flops 268435456 | bytes 4000000 | tf_op jit(solution)/shard_map/pallas_call | solution.py:551
  98.4 5.5 %collective-permute-done.14.refs_1_ = bf16[128,1024]{1,0:T(8,128)(2,1)S(1)} collective-permute-done((bf16[128,1024]{1,0:T(8,128)(2,1)}, bf16[128,1024]{1,0:T(8,128)(2,1)S(1)}, u32[]{:S(2)}, u32[]{:S(2)}) %collective-permute-start.14) | collective-permute-done | bytes 262176 | tf_op jit(solution)/shard_map/ppermute | solution.py:401
  105.5 5.0 %collective-permute-done.24.refs_11_ = bf16[256,1024]{1,0:T(8,128)(2,1)S(1)} collective-permute-done((bf16[256,1024]{1,0:T(8,128)(2,1)S(1)}, bf16[256,1024]{1,0:T(8,128)(2,1)S(1)}, u32[]{:S(2)}, u32[]{:S(2)}) %collective-permute-start.24) | collective-permute-done | bytes 524320 | tf_op jit(solution)/shard_map/ppermute | solution.py:408
  111.4 6.5 %shard_map.265 = (bf16[512,1024]{1,0:T(8,128)(2,1)}, bf16[1024,1024]{1,0:T(8,128)(2,1)}, bf16[1024,1024]{1,0:T(8,128)(2,1)}, f32[512,1024]{1,0:T(8,128)}, bf16[5...) custom-call(bf16[128,1024]{1,0:T(8,128)(2,1)} %get-tuple-element.61.refs_0_, ...), custom_call_target="tpu_custom_call" | custom-call | flops 2147483648 | bytes 16000000 | tf_op jit(solution)/shard_map/pallas_call | solution.py:564
  122.0 7.8 %collective-permute-done.26.from_seq = bf16[128,1024]{1,0:T(8,128)(2,1)S(1)} collective-permute-done((bf16[128,1024]{1,0:T(8,128)(2,1)S(1)}, bf16[128,1024]{1,0:T(8,128)(2,1)S(1)}, u32[]{:S(2)}, u32[]{:S(2)}) %collective-permute-start.26) | collective-permute-done | bytes 262176 | tf_op jit(solution)/shard_map/ppermute | solution.py:401
  130.4 3.1 %shard_map.266 = (bf16[128,1024]{1,0:T(8,128)(2,1)}, f32[128,1024]{1,0:T(8,128)}, bf16[128,1024]{1,0:T(8,128)(2,1)}, f32[8,1024]{1,0:T(8,128)}) custom-call(f32[128,1024]{1,0:T(8,128)} %get-tuple-element.60.first, f32[2,128,1024]{2,1,0:T(8,128)} %get-tuple-element.64.keep, bf16[2,128,1024]{2,1,0:T(8,128)(2,1)} %copy-done.6, bf16[128,1024]{1,0:T(8,128)(2,1)} %copy-done.25, ...), custom_call_target="tpu_custom_call" | custom-call | bytes 3000000 | tf_op jit(solution)/shard_map/pallas_call | solution.py:579
  134.1 7.2 %collective-permute-done.27.refs_1_ = bf16[128,1024]{1,0:T(8,128)(2,1)S(1)} collective-permute-done((bf16[128,1024]{1,0:T(8,128)(2,1)}, bf16[128,1024]{1,0:T(8,128)(2,1)S(1)}, u32[]{:S(2)}, u32[]{:S(2)}) %collective-permute-start.27) | collective-permute-done | bytes 262176 | tf_op jit(solution)/shard_map/ppermute | solution.py:401
  143.5 10.2 %shard_map.267 = (bf16[8,256,1024]{2,1,0:T(8,128)(2,1)}, f32[2,128,1024]{2,1,0:T(8,128)}, bf16[2,128,1024]{2,1,0:T(8,128)(2,1)}, f32[1,1024]{1,0:T(1,128)}) custom-call(bf16[128,1024]{1,0:T(8,128)(2,1)} %get-tuple-element.69.refs_0_, bf16[128,1024]{1,0:T(8,128)(2,1)} %copy-done.42, bf16[128,1024]{1,0:T(8,128)(2,1)} %copy-done.43, ...), custom_call_target="tpu_custom_call" | custom-call | flops 4294967296 | bytes 16000000 | tf_op jit(solution)/shard_map/pallas_call | solution.py:590
  157.2 11.9 %collective-permute-done.46 = bf16[256,1024]{1,0:T(8,128)(2,1)S(1)} collective-permute-done((bf16[256,1024]{1,0:T(8,128)(2,1)S(1)}, bf16[256,1024]{1,0:T(8,128)(2,1)S(1)}, u32[]{:S(2)}, u32[]{:S(2)}) %collective-permute-start.46) | collective-permute-done | bytes 524320 | tf_op jit(solution)/shard_map/ppermute | solution.py:421
  172.3 6.3 %collective-permute-done.31.from_seq = bf16[128,1024]{1,0:T(8,128)(2,1)S(1)} collective-permute-done((bf16[128,1024]{1,0:T(8,128)(2,1)S(1)}, bf16[128,1024]{1,0:T(8,128)(2,1)S(1)}, u32[]{:S(2)}, u32[]{:S(2)}) %collective-permute-start.31) | collective-permute-done | bytes 262176 | tf_op jit(solution)/shard_map/ppermute | solution.py:401
  179.3 5.2 %shard_map.268 = (f32[128,1024]{1,0:T(8,128)}, f32[1024,512]{1,0:T(8,128)}, bf16[1024,512]{1,0:T(8,128)(2,1)}, bf16[128,512]{1,0:T(8,128)(2,1)}, bf16[128,512]{1,0:T(8,128)(2,1)}, /*index=5*/f32[8,1024]{1,0:T(8,128)}) custom-call(f32[128,1024]{1,0:T(8,128)} %get-tuple-element.67.resid, f32[128,1024]{1,0:T(8,128)} %get-tuple-element.68.grad_two, ...), custom_call_target="tpu_custom_call" | custom-call | flops 536870912 | bytes 8000000 | tf_op jit(solution)/shard_map/pallas_call | solution.py:599
  190.7 9.9 %collective-permute-done.48 = bf16[256,1024]{1,0:T(8,128)(2,1)S(1)} collective-permute-done((bf16[256,1024]{1,0:T(8,128)(2,1)S(1)}, bf16[256,1024]{1,0:T(8,128)(2,1)S(1)}, u32[]{:S(2)}, u32[]{:S(2)}) %collective-permute-start.48) | collective-permute-done | bytes 524320 | tf_op jit(solution)/shard_map/ppermute | solution.py:421
  206.6 14.7 %shard_map.269 = (bf16[8,144,1280]{2,1,0:T(8,128)(2,1)}, f32[2,128,1024]{2,1,0:T(8,128)}, bf16[2,128,1024]{2,1,0:T(8,128)(2,1)}) custom-call(bf16[512,768]{1,0:T(8,128)(2,1)} %get-tuple-element.79.refs_0_, bf16[128,512]{1,0:T(8,128)(2,1)} %get-tuple-element.80.refs_1_, bf16[128,512]{1,0:T(8,128)(2,1)} %copy-done.23, bf16[256,256]{1,0:T(8,128)(2,1)} %copy-done.30, ...), custom_call_target="tpu_custom_call" | custom-call | flops 1610612736 | bytes 12000000 | tf_op jit(solution)/shard_map/pallas_call | solution.py:615
  226.2 7.3 %collective-permute-done.37 = bf16[144,1280]{1,0:T(8,128)(2,1)S(1)} collective-permute-done((bf16[144,1280]{1,0:T(8,128)(2,1)S(1)}, bf16[144,1280]{1,0:T(8,128)(2,1)S(1)}, u32[]{:S(2)}, u32[]{:S(2)}) %collective-permute-start.37) | collective-permute-done | bytes 368672 | tf_op jit(solution)/shard_map/ppermute | solution.py:421
  236.4 7.3 %collective-permute-done.38 = bf16[144,1280]{1,0:T(8,128)(2,1)S(1)} collective-permute-done((bf16[144,1280]{1,0:T(8,128)(2,1)S(1)}, bf16[144,1280]{1,0:T(8,128)(2,1)S(1)}, u32[]{:S(2)}, u32[]{:S(2)}) %collective-permute-start.38) | collective-permute-done | bytes 368672 | tf_op jit(solution)/shard_map/ppermute | solution.py:421
  245.9 7.0 %collective-permute-done.36 = bf16[128,1024]{1,0:T(8,128)(2,1)S(1)} collective-permute-done((bf16[128,1024]{1,0:T(8,128)(2,1)S(1)}, bf16[128,1024]{1,0:T(8,128)(2,1)S(1)}, u32[]{:S(2)}, u32[]{:S(2)}) %collective-permute-start.36) | collective-permute-done | bytes 262176 | tf_op jit(solution)/shard_map/ppermute | solution.py:401
  256.3 6.7 %collective-permute-done.40 = bf16[144,1280]{1,0:T(8,128)(2,1)S(1)} collective-permute-done((bf16[144,1280]{1,0:T(8,128)(2,1)S(1)}, bf16[144,1280]{1,0:T(8,128)(2,1)S(1)}, u32[]{:S(2)}, u32[]{:S(2)}) %collective-permute-start.40) | collective-permute-done | bytes 368672 | tf_op jit(solution)/shard_map/ppermute | solution.py:423
  269.0 9.3 %collective-permute-done.45 = bf16[144,1280]{1,0:T(8,128)(2,1)S(1)} collective-permute-done((bf16[144,1280]{1,0:T(8,128)(2,1)S(1)}, bf16[144,1280]{1,0:T(8,128)(2,1)S(1)}, u32[]{:S(2)}, u32[]{:S(2)}) %collective-permute-start.45) | collective-permute-done | bytes 368672 | tf_op jit(solution)/shard_map/ppermute | solution.py:401
  (271 shorter events, 91.4 us)
Async XLA Ops:
  10.4 14.2 %collective-permute-start.5 = (bf16[144,1280]{1,0:T(8,128)(2,1)S(1)}, bf16[144,1280]{1,0:T(8,128)(2,1)S(1)}, u32[]{:S(2)}, u32[]{:S(2)}) collective-permute-start(bf16[144,1280]{1,0:T(8,128)(2,1)S(1)} %fusion.14.refs_4_), channel_id=1, source_target_pairs={{0,4},{2,6},{8,0},{10,2},{16,8},{18,10},{24,16},{26,18},{28,24},{3... | collective-permute-start | bytes 1105928 | tf_op jit(solution)/shard_map/ppermute | solution.py:411
  23.1 18.6 %collective-permute-start = (bf16[128,1024]{1,0:T(8,128)(2,1)S(1)}, bf16[128,1024]{1,0:T(8,128)(2,1)S(1)}, u32[]{:S(2)}, u32[]{:S(2)}) collective-permute-start(bf16[128,1024]{1,0:T(8,128)(2,1)S(1)} %bitcast.183), channel_id=1, source_target_pairs={{0,1},{1,0},{2,3},{3,2},{4,5},{5,4},{6,7},{7,6},{8,9},{9,8},{10,11... | collective-permute-start | bytes 786440 | tf_op jit(solution)/shard_map/ppermute | solution.py:401
  24.7 15.0 %collective-permute-start.7 = (bf16[144,1280]{1,0:T(8,128)(2,1)S(1)}, bf16[144,1280]{1,0:T(8,128)(2,1)S(1)}, u32[]{:S(2)}, u32[]{:S(2)}) collective-permute-start(bf16[144,1280]{1,0:T(8,128)(2,1)S(1)} %collective-permute-done.5.refs_6_), channel_id=1, source_target_pairs={{0,4},{2,6},{8,0},{10,2},{16,8},{18,10},{24,16},{26,18},{28,24},{3... | collective-permute-start | bytes 1105928 | tf_op jit(solution)/shard_map/ppermute | solution.py:411
  38.6 30.6 %collective-permute-start.18 = (bf16[256,1024]{1,0:T(8,128)(2,1)S(1)}, bf16[256,1024]{1,0:T(8,128)(2,1)S(1)}, u32[]{:S(2)}, u32[]{:S(2)}) collective-permute-start(bf16[256,1024]{1,0:T(8,128)(2,1)S(1)} %pad_maximum_fusion.refs_4_), channel_id=1, source_target_pairs={{0,4},{2,6},{8,0},{10,2},{16,8},{18,10},{24,16},{26,18},{28,24},{3... | collective-permute-start | bytes 1572872 | tf_op jit(solution)/shard_map/ppermute | solution.py:408
  39.7 18.4 %collective-permute-start.9 = (bf16[144,1280]{1,0:T(8,128)(2,1)S(1)}, bf16[144,1280]{1,0:T(8,128)(2,1)S(1)}, u32[]{:S(2)}, u32[]{:S(2)}) collective-permute-start(bf16[144,1280]{1,0:T(8,128)(2,1)S(1)} %collective-permute-done.7.refs_8_), channel_id=1, source_target_pairs={{0,4},{2,6},{8,0},{10,2},{16,8},{18,10},{24,16},{26,18},{28,24},{3... | collective-permute-start | bytes 1105928 | tf_op jit(solution)/shard_map/ppermute | solution.py:411
  41.3 16.9 %collective-permute-start.10 = (bf16[144,1280]{1,0:T(8,128)(2,1)S(1)}, bf16[144,1280]{1,0:T(8,128)(2,1)S(1)}, u32[]{:S(2)}, u32[]{:S(2)}) collective-permute-start(bf16[144,1280]{1,0:T(8,128)(2,1)S(1)} %collective-permute-done.8.refs_9_), channel_id=1, source_target_pairs={{0,8},{2,10},{8,16},{10,18},{16,24},{18,26},{24,28},{26,30},{28,20... | collective-permute-start | bytes 1105928 | tf_op jit(solution)/shard_map/ppermute | solution.py:408
  43.3 26.7 %collective-permute-start.19 = (bf16[256,1024]{1,0:T(8,128)(2,1)S(1)}, bf16[256,1024]{1,0:T(8,128)(2,1)S(1)}, u32[]{:S(2)}, u32[]{:S(2)}) collective-permute-start(bf16[256,1024]{1,0:T(8,128)(2,1)S(1)} %pad_maximum_fusion.refs_4_), channel_id=1, source_target_pairs={{0,8},{2,10},{8,16},{10,18},{16,24},{18,26},{24,28},{26,30},{28,20... | collective-permute-start | bytes 1572872 | tf_op jit(solution)/shard_map/ppermute | solution.py:411
  69.1 21.8 %collective-permute-start.13 = (bf16[1024,512]{1,0:T(8,128)(2,1)}, bf16[1024,512]{1,0:T(8,128)(2,1)S(1)}, u32[]{:S(2)}, u32[]{:S(2)}) collective-permute-start(bf16[1024,512]{1,0:T(8,128)(2,1)} %get-tuple-element.58.mine), channel_id=1, source_target_pairs={{0,2},{2,0},{4,6},{6,4},{8,10},{10,8},{12,14},{14,12},{16,18},{18,... | collective-permute-start | bytes 3145736 | tf_op jit(solution)/shard_map/ppermute | solution.py:398
  69.2 14.3 %collective-permute-start.20 = (bf16[256,1024]{1,0:T(8,128)(2,1)S(1)}, bf16[256,1024]{1,0:T(8,128)(2,1)S(1)}, u32[]{:S(2)}, u32[]{:S(2)}) collective-permute-start(bf16[256,1024]{1,0:T(8,128)(2,1)S(1)} %collective-permute-done.18.refs_5_), channel_id=1, source_target_pairs={{0,4},{2,6},{8,0},{10,2},{16,8},{18,10},{24,16},{26,18},{28,24},{3... | collective-permute-start | bytes 1572872 | tf_op jit(solution)/shard_map/ppermute | solution.py:408
  70.0 19.6 %collective-permute-start.21 = (bf16[256,1024]{1,0:T(8,128)(2,1)S(1)}, bf16[256,1024]{1,0:T(8,128)(2,1)S(1)}, u32[]{:S(2)}, u32[]{:S(2)}) collective-permute-start(bf16[256,1024]{1,0:T(8,128)(2,1)S(1)} %collective-permute-done.19.refs_6_), channel_id=1, source_target_pairs={{0,8},{2,10},{8,16},{10,18},{16,24},{18,26},{24,28},{26,30},{28,20... | collective-permute-start | bytes 1572872 | tf_op jit(solution)/shard_map/ppermute | solution.py:411
  89.6 14.4 %collective-permute-start.23 = (bf16[256,1024]{1,0:T(8,128)(2,1)S(1)}, bf16[256,1024]{1,0:T(8,128)(2,1)S(1)}, u32[]{:S(2)}, u32[]{:S(2)}) collective-permute-start(bf16[256,1024]{1,0:T(8,128)(2,1)S(1)} %collective-permute-done.21.refs_8_), channel_id=1, source_target_pairs={{0,8},{2,10},{8,16},{10,18},{16,24},{18,26},{24,28},{26,30},{28,20... | collective-permute-start | bytes 1572872 | tf_op jit(solution)/shard_map/ppermute | solution.py:411
  155.1 14.0 %collective-permute-start.46 = (bf16[256,1024]{1,0:T(8,128)(2,1)S(1)}, bf16[256,1024]{1,0:T(8,128)(2,1)S(1)}, u32[]{:S(2)}, u32[]{:S(2)}) collective-permute-start(bf16[256,1024]{1,0:T(8,128)(2,1)S(1)} %get-tuple-element.101), channel_id=1, source_target_pairs={{0,8},{2,10},{8,16},{10,18},{16,24},{18,26},{24,28},{26,30},{28,20... | collective-permute-start | bytes 1572872 | tf_op jit(solution)/shard_map/ppermute | solution.py:421
  156.0 15.3 %collective-permute-start.30 = (bf16[2,128,1024]{2,1,0:T(8,128)(2,1)}, bf16[2,128,1024]{2,1,0:T(8,128)(2,1)S(1)}, u32[]{:S(2)}, u32[]{:S(2)}) collective-permute-start(bf16[2,128,1024]{2,1,0:T(8,128)(2,1)} %get-tuple-element.76), channel_id=1, source_target_pairs={{0,2},{2,0},{4,6},{6,4},{8,10},{10,8},{12,14},{14,12},{16,18},{18,... | collective-permute-start | bytes 1572872 | tf_op jit(solution)/shard_map/ppermute | solution.py:398
  156.0 28.6 %collective-permute-start.50 = (bf16[256,1024]{1,0:T(8,128)(2,1)S(1)}, bf16[256,1024]{1,0:T(8,128)(2,1)S(1)}, u32[]{:S(2)}, u32[]{:S(2)}) collective-permute-start(bf16[256,1024]{1,0:T(8,128)(2,1)S(1)} %get-tuple-element.102), channel_id=1, source_target_pairs={{0,4},{2,6},{8,0},{10,2},{16,8},{18,10},{24,16},{26,18},{28,24},{3... | collective-permute-start | bytes 1572872 | tf_op jit(solution)/shard_map/ppermute | solution.py:421
  170.4 14.3 %collective-permute-start.47 = (bf16[256,1024]{1,0:T(8,128)(2,1)S(1)}, bf16[256,1024]{1,0:T(8,128)(2,1)S(1)}, u32[]{:S(2)}, u32[]{:S(2)}) collective-permute-start(bf16[256,1024]{1,0:T(8,128)(2,1)S(1)} %fusion.5), channel_id=1, source_target_pairs={{0,8},{2,10},{8,16},{10,18},{16,24},{18,26},{24,28},{26,30},{28,20... | collective-permute-start | bytes 1572872 | tf_op jit(solution)/shard_map/ppermute | solution.py:421
  184.5 21.1 %collective-permute-start.34 = (bf16[1024,512]{1,0:T(8,128)(2,1)}, bf16[1024,512]{1,0:T(8,128)(2,1)S(1)}, u32[]{:S(2)}, u32[]{:S(2)}) collective-permute-start(bf16[1024,512]{1,0:T(8,128)(2,1)} %get-tuple-element.85), channel_id=1, source_target_pairs={{0,2},{2,0},{4,6},{6,4},{8,10},{10,8},{12,14},{14,12},{16,18},{18,... | collective-permute-start | bytes 3145736 | tf_op jit(solution)/shard_map/ppermute | solution.py:398
  186.3 14.3 %collective-permute-start.48 = (bf16[256,1024]{1,0:T(8,128)(2,1)S(1)}, bf16[256,1024]{1,0:T(8,128)(2,1)S(1)}, u32[]{:S(2)}, u32[]{:S(2)}) collective-permute-start(bf16[256,1024]{1,0:T(8,128)(2,1)S(1)} %get-tuple-element.99), channel_id=1, source_target_pairs={{0,8},{2,10},{8,16},{10,18},{16,24},{18,26},{24,28},{26,30},{28,20... | collective-permute-start | bytes 1572872 | tf_op jit(solution)/shard_map/ppermute | solution.py:421
  187.9 14.0 %collective-permute-start.51 = (bf16[256,1024]{1,0:T(8,128)(2,1)S(1)}, bf16[256,1024]{1,0:T(8,128)(2,1)S(1)}, u32[]{:S(2)}, u32[]{:S(2)}) collective-permute-start(bf16[256,1024]{1,0:T(8,128)(2,1)S(1)} %get-tuple-element.100), channel_id=1, source_target_pairs={{0,4},{2,6},{8,0},{10,2},{16,8},{18,10},{24,16},{26,18},{28,24},{3... | collective-permute-start | bytes 1572872 | tf_op jit(solution)/shard_map/ppermute | solution.py:421
  189.7 15.9 %collective-permute-start.33 = (bf16[256,256]{1,0:T(8,128)(2,1)S(1)}, bf16[256,256]{1,0:T(8,128)(2,1)S(1)}, u32[]{:S(2)}, u32[]{:S(2)}) collective-permute-start(bf16[256,256]{1,0:T(8,128)(2,1)S(1)} %pad_maximum_fusion.8), channel_id=1, source_target_pairs={{0,1},{1,0},{2,3},{3,2},{4,5},{5,4},{6,7},{7,6},{8,9},{9,8},{10,11... | collective-permute-start | bytes 393224 | tf_op jit(solution)/shard_map/ppermute | solution.py:401
  203.5 21.2 %collective-permute-start.49 = (bf16[256,1024]{1,0:T(8,128)(2,1)S(1)}, bf16[256,1024]{1,0:T(8,128)(2,1)S(1)}, u32[]{:S(2)}, u32[]{:S(2)}) collective-permute-start(bf16[256,1024]{1,0:T(8,128)(2,1)S(1)} %get-tuple-element.97), channel_id=1, source_target_pairs={{0,8},{2,10},{8,16},{10,18},{16,24},{18,26},{24,28},{26,30},{28,20... | collective-permute-start | bytes 1572872 | tf_op jit(solution)/shard_map/ppermute | solution.py:423
  205.1 19.5 %collective-permute-start.52 = (bf16[256,1024]{1,0:T(8,128)(2,1)S(1)}, bf16[256,1024]{1,0:T(8,128)(2,1)S(1)}, u32[]{:S(2)}, u32[]{:S(2)}) collective-permute-start(bf16[256,1024]{1,0:T(8,128)(2,1)S(1)} %get-tuple-element.98), channel_id=1, source_target_pairs={{0,4},{2,6},{8,0},{10,2},{16,8},{18,10},{24,16},{26,18},{28,24},{3... | collective-permute-start | bytes 1572872 | tf_op jit(solution)/shard_map/ppermute | solution.py:423
  221.3 13.9 %collective-permute-start.35 = (bf16[2,128,1024]{2,1,0:T(8,128)(2,1)}, bf16[2,128,1024]{2,1,0:T(8,128)(2,1)S(1)}, u32[]{:S(2)}, u32[]{:S(2)}) collective-permute-start(bf16[2,128,1024]{2,1,0:T(8,128)(2,1)} %get-tuple-element.90), channel_id=1, source_target_pairs={{0,2},{2,0},{4,6},{6,4},{8,10},{10,8},{12,14},{14,12},{16,18},{18,... | collective-permute-start | bytes 1572872 | tf_op jit(solution)/shard_map/ppermute | solution.py:398
  234.1 19.7 %collective-permute-start.54 = (bf16[256,1024]{1,0:T(8,128)(2,1)S(1)}, bf16[256,1024]{1,0:T(8,128)(2,1)S(1)}, u32[]{:S(2)}, u32[]{:S(2)}) collective-permute-start(bf16[256,1024]{1,0:T(8,128)(2,1)S(1)} %pad_maximum_fusion.1), channel_id=1, source_target_pairs={{0,1},{1,0},{2,3},{3,2},{4,5},{5,4},{6,7},{7,6},{8,9},{9,8},{10,11... | collective-permute-start | bytes 1572872 | tf_op jit(solution)/shard_map/ppermute | solution.py:401
  235.3 17.6 %collective-permute-start.36 = (bf16[128,1024]{1,0:T(8,128)(2,1)S(1)}, bf16[128,1024]{1,0:T(8,128)(2,1)S(1)}, u32[]{:S(2)}, u32[]{:S(2)}) collective-permute-start(bf16[128,1024]{1,0:T(8,128)(2,1)S(1)} %fusion.17), channel_id=1, source_target_pairs={{0,1},{1,0},{2,3},{3,2},{4,5},{5,4},{6,7},{7,6},{8,9},{9,8},{10,11... | collective-permute-start | bytes 786440 | tf_op jit(solution)/shard_map/ppermute | solution.py:401
  (77 other events, 882.0 us)
where the time goes:
time: 284 us
  waiting for transfers between devices  152 us (54%)
  Pallas kernels  54.6 us (19%)
  starting transfers between devices  42.1 us (15%)
  local copies, waits for them, and re-layouts  19.8 us (7%)
  other arithmetic  13.4 us (5%)
    ppermute x10, waiting for transfers between devices, swap_seq(): return lax.ppermute(array, 'seq', [(0, 1), (1, 0)])  45.9 us
    ppermute x8, waiting for transfers between devices, gather_ring(): one = lax.ppermute(one, 'dp', far)  38.1 us
    ppermute x10, waiting for transfers between devices, run(): moving = lax.ppermute(moving, 'dp', perm)  37.6 us
    pallas_call x1, Pallas kernels, per_device(): call(functools.partial(attention_back_kernel, micro, where_one), [((PARTS...  14.7 us
    ppermute x6, waiting for transfers between devices, gather_ring(): two = lax.ppermute(two, 'dp', near)  13.9 us
    ppermute x8, starting transfers between devices, gather_ring(): one = lax.ppermute(one, 'dp', far)  10.8 us
    ppermute x10, starting transfers between devices, swap_seq(): return lax.ppermute(array, 'seq', [(0, 1), (1, 0)])  10.5 us
    pallas_call x1, Pallas kernels, per_device(): call(functools.partial(backward_kernel, micro, where_two), [((PARTS, 256,...  10.2 us
  transfers between devices with their start and end apart: 55, of which 27 were waited for; matrix products, arithmetic and copies ran while one was open for 5% of the time, Pallas kernels for 12%

commit v1 on v0

--- a/solution.py
+++ b/solution.py
@@ -13,7 +13,8 @@
 PARTS = 8
 SHORT = jnp.bfloat16
 WIDE = jnp.float32
-LIMIT = 56 * 1024 * 1024
+LIMIT = 24 * 1024 * 1024
+WHOLE = 56 * 1024 * 1024
 LINES = 16
 LANES = 256
 
@@ -88,12 +89,12 @@
     return jnp.where(spot < half, 2 * spot, 2 * (chips - 1 - spot) + 1)
 
 
-def call(body, outs, scratch=(), flops=0, moved=0):
+def call(body, outs, scratch=(), flops=0, moved=0, limit=LIMIT):
     return pl.pallas_call(
         body,
         out_shape=[jax.ShapeDtypeStruct(shape, kind) for shape, kind in outs],
         scratch_shapes=[pltpu.VMEM(shape, kind) for shape, kind in scratch],
-        compiler_params=pltpu.CompilerParams(vmem_limit_bytes=LIMIT),
+        compiler_params=pltpu.CompilerParams(vmem_limit_bytes=limit),
         cost_estimate=pl.CostEstimate(flops=flops, bytes_accessed=moved, transcendentals=0),
     )
 
@@ -143,20 +144,28 @@
 
 
 def attention_kernel(micro, where, *refs):
-    pieces, chunks, rest = refs[:4], refs[4:12], refs[12:]
-    tokens, full, qkv, keep, send, vectors, up_bias, out_half, wide = rest
+    pieces, chunks, rest = refs[:4], refs[4:13], refs[13:]
+    tokens, full, qkv, keep, send, kept, vectors, up_bias, out_half, wide = rest
     chip, core, half = here()
     quarter = keep.shape[1]
     scale = 1.0 / math.sqrt(HEAD)
     fill_group(tokens, pieces, micro)
     for step in range(PARTS):
         spot = block(where(step, chip), 128)
-        chunk = chunks[step]
-        full[spot, :] = chunk[:128, : 3 * quarter]
-        out_half[spot, :] = chunk[:128, 3 * quarter :]
-        lines = jnp.concatenate([chunk[128:, :64], chunk[128:, LANES : LANES + 64]], axis=1)
+        chunk, start = chunks[step], 128
+        if step < PARTS - 1:
+            full[spot, :] = chunk[:128, : 3 * quarter]
+            out_half[spot, :] = chunk[:128, 3 * quarter :]
+        else:
+            for side in range(2):
+                piece = chunks[step + side]
+                inner = block(2 * where(step, chip) + side, 64)
+                full[inner, :] = piece[:64, : 3 * quarter]
+                out_half[inner, :] = piece[:64, 3 * quarter :]
+            chunk, start = piece, 64
+        lines = jnp.concatenate([chunk[start:, :64], chunk[start:, LANES : LANES + 64]], axis=1)
         vectors[:, spot] = lines.astype(WIDE)
-        lines = chunk[128:, block(core * (LANES // 128) + half, 128)]
+        lines = chunk[start:, block(core * (LANES // 128) + half, 128)]
         up_bias[:, spot] = lines.astype(WIDE)[8:9, :]
     wide[...] = times(tokens[...], full[...])
     spot = block(2 * half + core, quarter)
@@ -172,8 +181,9 @@
                 queries, keys, values = heads_of(
                     qkv, slice(item * length, (item + 1) * length), head, quarter
                 )
-                probs = softmax(queries, keys, scale).astype(SHORT)
-                both.append(times(probs, values))
+                probs = softmax(queries, keys, scale)
+                kept[item * (quarter // HEAD) + head] = probs
+                both.append(times(probs.astype(SHORT), values))
             both = jnp.concatenate(both, axis=1).astype(SHORT)
             spot = slice(pair * 128, (pair + 1) * 128)
             keep[item * rows : (item + 1) * rows, spot] = both[:rows]
@@ -217,14 +227,15 @@
 
 
 def forward_kernel(micro, where, *refs):
-    pieces, chunks, up_bias, rest = refs[:4], refs[4:12], refs[12], refs[13:]
+    pieces, chunks, up_bias, rest = refs[:4], refs[4:22], refs[22], refs[23:]
     group, full_up, full_down, pre_act, act, keep, send = rest
     chip, _, _ = here()
     fill_group(group, pieces, micro)
-    for step in range(PARTS):
-        spot = block(where(step, chip), 128)
-        full_up[spot, :] = chunks[step][:128, :]
-        full_down[spot, :] = chunks[step][128:, :]
+    for full, parts in ((full_up, chunks[:9]), (full_down, chunks[9:])):
+        for step in range(PARTS - 1):
+            full[block(where(step, chip), 128), :] = parts[step][...]
+        for side in range(2):
+            full[block(2 * where(PARTS - 1, chip) + side, 64), :] = parts[PARTS - 1 + side][...]
     rows = pieces[0].shape[0] // micro
     tall = group.shape[0] // 2
     for side in range(2):
@@ -234,6 +245,11 @@
         act[spot, :] = gelu_exact(pre).astype(SHORT)
         out = times(act[spot, :], full_down[...])
         split_rows(out, side * tall, micro, rows, keep, send)
+
+
+def slope_kernel(pre_act, slope):
+    for start in range(0, pre_act.shape[0], 64):
+        slope[start : start + 64, :] = gelu_slope(pre_act[start : start + 64, :])
 
 
 def second_kernel(
@@ -255,7 +271,7 @@
 
 def backward_kernel(micro, where, *refs):
     pieces, rest = refs[:4], refs[4:]
-    group, full_up, full_down, pre_act, act, chunks, keep, send, sums, grad, pre = rest
+    group, full_up, full_down, slopes, act, chunks_up, chunks_down, keep, send, sums, grad, pre = rest
     chip, _, _ = here()
     fill_group(grad, pieces, micro)
     rows = pieces[0].shape[0] // micro
@@ -263,16 +279,15 @@
     total = None
     for side in range(2):
         spot = slice(side * tall, (side + 1) * tall)
-        slope = gelu_slope(pre_act[spot, :])
-        part = (times_back(grad[spot, :], full_down[...]) * slope).astype(SHORT)
+        part = (times_back(grad[spot, :], full_down[...]) * slopes[spot, :]).astype(SHORT)
         pre[spot, :] = part
         part = column_sum(part.astype(WIDE))
         total = part if total is None else total + part
     sums[...] = total
     for step in range(PARTS):
         spot = block(where(step, chip), 128)
-        chunks[step, 128:, :] = inner_rows(act[:, spot], grad[...]).astype(SHORT)
-        chunks[step, :128, :] = inner_rows(group[:, spot], pre[...]).astype(SHORT)
+        chunks_down[step] = inner_rows(act[:, spot], grad[...]).astype(SHORT)
+        chunks_up[step] = inner_rows(group[:, spot], pre[...]).astype(SHORT)
     for side in range(2):
         spot = slice(side * tall, (side + 1) * tall)
         out = times_back(pre[spot, :], full_up[...])
@@ -321,8 +336,8 @@
 
 
 def attention_back_kernel(micro, where, *refs):
-    qkv, ctx_keep, ctx_core, ctx_seq, tokens, full, out_keep, out_core = refs[:8]
-    sums_two, sums_one, up_sums, chunks, keep, send, grad, vectors = refs[8:]
+    qkv, kept, ctx_keep, ctx_core, ctx_seq, tokens, out_keep, out_core = refs[:8]
+    sums_two, sums_one, up_sums, chunks, grad, flag, vectors = refs[8:]
     chip, core, half = here()
     quarter = qkv.shape[1] // 3
     length = qkv.shape[0] // (2 * micro)
@@ -339,7 +354,7 @@
             results = [[], [], []]
             for side in range(2):
                 queries, keys, values = heads_of(qkv, spot, 2 * pair + side, quarter)
-                probs = softmax(queries, keys, scale)
+                probs = kept[item * (quarter // HEAD) + 2 * pair + side]
                 own = incoming[:, side * HEAD : (side + 1) * HEAD]
                 grad_probs = times_back(own, values)
                 along = jnp.sum(probs * grad_probs, axis=-1, keepdims=True)
@@ -359,6 +374,7 @@
     vectors[2:5, :] = sums_one[0:3, :]
     vectors[5:8, :] = sums_two[0:3, :]
     vectors[8:9, :] = up_sums[...]
+    flag[...] = vectors[0:8, 0:128]
     for step in range(PARTS):
         spot = block(where(step, chip), 128)
         chunks[step, :128, : 3 * quarter] = inner_rows(tokens[:, spot], grad[...]).astype(SHORT)
@@ -370,10 +386,19 @@
         chunks[step, 128:, :64] = lines[:, :64]
         chunks[step, 128:, LANES : LANES + 64] = lines[:, 64:]
         chunks[step, 128:, 2 * LANES : 2 * LANES + 128] = lines
-    tall = tokens.shape[0] // 2
+
+
+def input_back_kernel(micro, rows, grad, full, keep, send):
+    tall = grad.shape[0] // 2
     for side in range(2):
         out = times_back(grad[side * tall : (side + 1) * tall, :], full[...])
         split_rows(out, side * tall, micro, rows, keep, send)
+
+
+def after(gate, *values):
+    if gate is None:
+        return values
+    return lax.optimization_barrier((*values, gate))[:-1]
 
 
 def build(mesh):
@@ -400,31 +425,39 @@
     def swap_seq(array):
         return lax.ppermute(array, "seq", [(0, 1), (1, 0)])
 
-    def gather_ring(chunk, flip):
+    def gather_ring(chunk, cut, flip, gates=(None, None, None)):
         far, near = (backward, onward) if flip else (onward, backward)
         got = [chunk]
         one = two = chunk
-        for step in range(1, chips // 2 + 1):
+        for step in range(chips // 2 - 1):
+            if step:
+                one, two = after(gates[step - 1], one, two)
             one = lax.ppermute(one, "dp", far)
-            got.append(one)
-            if step < chips // 2:
-                two = lax.ppermute(two, "dp", near)
-                got.append(two)
-        return got
-
-    def sum_ring(parts, flip):
+            two = lax.ppermute(two, "dp", near)
+            got += [one, two]
+        one, two = after(gates[-1], one, two)
+        return got + [lax.ppermute(one[:cut], "dp", far), lax.ppermute(two[cut:], "dp", near)]
+
+    def sum_ring(parts, cut, flip, gates=(None, None, None)):
         far, near = (onward, backward) if flip else (backward, onward)
-
-        def run(perm, steps):
-            moving = parts[steps[0]]
-            for step in steps[1:]:
-                moving = lax.ppermute(moving, "dp", perm)
-                moving = (moving.astype(WIDE) + parts[step].astype(WIDE)).astype(SHORT)
-            return lax.ppermute(moving, "dp", perm).astype(WIDE)
-
-        long = list(range(chips - 1, 0, -2))
-        short = list(range(chips - 2, 0, -2))
-        return run(far, long) + run(near, short) + parts[0].astype(WIDE)
+        last = parts[chips - 1]
+        one, two = last[:cut], last[cut:]
+        for step in range(chips // 2 - 1):
+            one = lax.ppermute(one, "dp", far)
+            two = lax.ppermute(two, "dp", near)
+            one, two = after(gates[step], one, two)
+            one, two = one.astype(WIDE), two.astype(WIDE)
+            place = chips - 3 - 2 * step
+            here, there = parts[place].astype(WIDE), parts[place + 1].astype(WIDE)
+            if step:
+                one, two = one + here, two + there
+            else:
+                one = jnp.concatenate([one + here[:cut], here[cut:]], axis=0)
+                two = jnp.concatenate([there[:cut], two + there[cut:]], axis=0)
+            one, two = one.astype(SHORT), two.astype(SHORT)
+        one = lax.ppermute(one, "dp", far)
+        two = lax.ppermute(two, "dp", near)
+        return one.astype(WIDE) + two.astype(WIDE) + parts[0].astype(WIDE)
 
     def where(flip, step, chip):
         return part_index(step, flip, ringed, chip, chips)
@@ -481,7 +514,7 @@
             shift_two,
             bias_up,
         )
-        mine, theirs = call(pack_kernel, [((depth + LINES, side), SHORT)] * 2, moved=10**6)(
+        mine, theirs = call(pack_kernel, [((depth + LINES, side), SHORT)] * 2, moved=10**6, limit=WHOLE)(
             *[vector.reshape(1, -1) for vector in vectors], w_qkv, w_out
         )
         theirs = swap_core(theirs)
@@ -496,12 +529,13 @@
         theirs = pick(by_unit, 1 - core, 2).reshape(depth, tall // 4)
         both = in_order(core, mine, swap_core(theirs), 0).reshape(2 * depth, tall // 4)
         own_down = pick(w_down.reshape(2, units // 2, width), half, 0)
-        chunk_two = jnp.concatenate([both, own_down], axis=0)
-
+        chunk_two, chunk_three = both, own_down
+
+        flat = inputs.reshape(own_rows, width)
+        shared = share(flat)
         if ringed:
-            chunks_one = gather_ring(chunk_one, False)
-            chunk_two, _ = lax.optimization_barrier((chunk_two, chunks_one[5]))
-            chunks_two = gather_ring(chunk_two, True)
+            chunks_one = gather_ring(chunk_one, 64, False, (chunk_two, shared[1], None))
+            chunk_two, chunk_three = after(chunks_one[5], chunk_two, chunk_three)
         else:
             whole = lax.all_gather(chunk_one, "dp", axis_index_groups=same_core)
             square = whole[:, : 2 * depth].reshape(PARTS, 128, side)
@@ -515,19 +549,16 @@
             lines = jnp.concatenate([slim, jnp.tile(bias, (1, 1, 2 * LANES // 128))], axis=1)
             lines = jnp.pad(lines, ((0, 0), (0, LINES - 9), (0, side - 2 * LANES)))
             whole = jnp.concatenate([square, lines], axis=1)
-            chunks_one = [whole[step] for step in range(PARTS)]
-            whole = lax.all_gather(chunk_two, "dp", axis_index_groups=same_core)
-            whole = jnp.concatenate(
-                [
-                    whole[:, : 2 * depth].reshape(PARTS, 128, width),
-                    whole[:, 2 * depth :].reshape(PARTS, 128, width),
-                ],
-                axis=1,
-            )
-            chunks_two = [whole[step] for step in range(PARTS)]
-
-        flat = inputs.reshape(own_rows, width)
-        tokens, full_qkv, qkv, ctx_keep, ctx_send, table, up_bias, out_mine = call(
+            chunks_one = [whole[step] for step in range(PARTS - 1)]
+            chunks_one += [whole[-1, :64], whole[-1, 64:]]
+            chunks_two = []
+            for chunk in (chunk_two, chunk_three):
+                whole = lax.all_gather(chunk, "dp", axis_index_groups=same_core)
+                whole = whole.reshape(PARTS, 128, width)
+                chunks_two += [whole[step] for step in range(PARTS - 1)]
+                chunks_two += [whole[-1, :64], whole[-1, 64:]]
+
+        tokens, full_qkv, qkv, ctx_keep, ctx_send, probs, table, up_bias, out_mine = call(
             functools.partial(attention_kernel, micro, where_one),
             [
                 ((group, width), SHORT),
@@ -535,6 +566,7 @@
                 ((group, 3 * quarter), SHORT),
                 ((group // 2, quarter), SHORT),
                 ((group // 2, quarter), SHORT),
+                ((2 * micro * quarter // HEAD, 2 * rows, 2 * rows), WIDE),
                 ((LINES, width), WIDE),
                 ((1, tall // 4), WIDE),
                 ((width, width // 2), SHORT),
@@ -542,7 +574,7 @@
             [((group, 3 * quarter), WIDE)],
             flops=2 * group * width * width,
             moved=8 * 10**6,
-        )(*share(flat), *chunks_one)
+        )(*shared, *chunks_one)
         out_other = swap_core(out_mine)
         ctx_seq = swap_seq(ctx_send)
         ctx_core = swap_core(
@@ -560,6 +592,11 @@
             moved=4 * 10**6,
         )(flat, ctx_keep, ctx_seq, ctx_core, out_mine, out_other, table)
 
+        pieces = share(first_low)
+        if ringed:
+            gates = (ctx_seq, pieces[1], None)
+            chunks_two = gather_ring(chunk_two, 64, True, gates)
+            chunks_two += gather_ring(chunk_three, 64, True, gates)
         split_out = [((2, own_rows, width), WIDE), ((2, own_rows, width), SHORT)]
         first_group, full_up, full_down, pre_act, act, keep, send = call(
             functools.partial(forward_kernel, micro, where_two),
@@ -573,9 +610,12 @@
             + split_out,
             flops=group * width * tall,
             moved=16 * 10**6,
-        )(*share(first_low), *chunks_two, up_bias)
+        )(*pieces, *chunks_two, up_bias)
         from_core = swap_core(send)
-        from_seq = finish_sum(keep, from_core)
+        moving = (keep[1] + from_core[1].astype(WIDE)).astype(SHORT)
+        (pre_act,) = after(moving, pre_act)
+        (slopes,) = call(slope_kernel, [((group, tall // 4), WIDE)], moved=5 * 10**6)(pre_act)
+        from_seq = swap_seq(moving)
         layer_out, grad_two, mlp_low, sums_two = call(
             second_kernel,
             [
@@ -587,15 +627,16 @@
             moved=3 * 10**6,
         )(first, keep, from_core, from_seq, table, cotangent.reshape(own_rows, width))
 
-        grads_two, keep, send, up_sums = call(
+        grads_two, grads_three, keep, send, up_sums = call(
             functools.partial(backward_kernel, micro, where_two),
-            [((PARTS, 256, width), SHORT)] + split_out + [((1, tall // 4), WIDE)],
+            [((PARTS, 128, width), SHORT)] * 2 + split_out + [((1, tall // 4), WIDE)],
             [((group, width), SHORT), ((group, tall // 4), SHORT)],
             flops=2 * group * width * tall,
             moved=16 * 10**6,
-        )(*share(mlp_low), first_group, full_up, full_down, pre_act, act)
+        )(*share(mlp_low), first_group, full_up, full_down, slopes, act)
         from_core = swap_core(send)
         from_seq = finish_sum(keep, from_core)
+        gate_one = from_seq
         grad_one, out_keep, out_send, grad_keep, grad_send, sums_one = call(
             first_back_kernel,
             [
@@ -612,40 +653,49 @@
         grad_core = swap_core(grad_send)
         grad_seq = swap_seq(jnp.concatenate([grad_keep[:, quarter:], grad_core[:, quarter:]]))
         out_core = swap_core(out_send)
-        grads_one, keep, send = call(
+        grads_one, grad_tokens, flag = call(
             functools.partial(attention_back_kernel, micro, where_one),
-            [((PARTS, 128 + LINES, side), SHORT)] + split_out,
-            [((group, 3 * quarter), SHORT), ((LINES, width), WIDE)],
+            [
+                ((PARTS, 128 + LINES, side), SHORT),
+                ((group, 3 * quarter), SHORT),
+                ((8, 128), WIDE),
+            ],
+            [((LINES, width), WIDE)],
             flops=3 * group * width * width,
             moved=12 * 10**6,
         )(
             qkv,
+            probs,
             grad_keep,
             grad_core,
             grad_seq,
             tokens,
-            full_qkv,
             out_keep,
             out_core,
             sums_two,
             sums_one,
             up_sums,
         )
+        keep, send = call(
+            functools.partial(input_back_kernel, micro, rows),
+            split_out,
+            flops=group * width * width,
+            moved=5 * 10**6,
+        )(grad_tokens, full_qkv)
         from_core = swap_core(send)
-        from_seq = finish_sum(keep, from_core)
+        moving = (keep[1] + from_core[1].astype(WIDE)).astype(SHORT)
+        from_seq = swap_seq(moving)
+        gates_one = (moving, from_seq, None)
         input_grad = grad_one + (keep[0] + from_core[0].astype(WIDE) + from_seq.astype(WIDE))
 
         if ringed:
-            share_two = sum_ring(grads_two, True)
-            share_one = sum_ring(grads_one, False)
+            share_three = sum_ring(grads_three, 64, True, (gate_one, flag, None))
+            share_two = sum_ring(grads_two, 64, True, (gate_one, flag, None))
+            share_one = sum_ring(grads_one, 64, False, gates_one)
         else:
-            whole = jnp.concatenate(
-                [
-                    grads_two[:, :128].reshape(chips, 2 * depth, width),
-                    grads_two[:, 128:].reshape(chips, units // 2, width),
-                ],
-                axis=1,
-            )
+            whole = grads_three.reshape(chips, units // 2, width)
+            share_three = lax.psum_scatter(whole, "dp", axis_index_groups=same_core).astype(WIDE)
+            whole = grads_two.reshape(chips, 2 * depth, width)
             share_two = lax.psum_scatter(whole, "dp", axis_index_groups=same_core).astype(WIDE)
             square = grads_one[:, :128].reshape(chips, 2 * depth, side)
             slim = grads_one[:, 128 : 128 + 8, : 2 * LANES].reshape(PARTS, 8, 2, LANES)[..., :64]
@@ -663,17 +713,10 @@
 
         split = share_two[: 2 * depth].reshape(2, depth, width).astype(SHORT)
         own, other = pick(split, core, 0), swap_core(pick(split, 1 - core, 0))
-        own_down = share_two[2 * depth :].astype(SHORT)
-        moved = swap_seq(jnp.concatenate([own, other, own_down], axis=0))
-        by_chip = (depth, chips, units // 2)
-        near = in_order(core, own.reshape(by_chip), other.reshape(by_chip), 2)
-        away = in_order(
-            core, moved[:depth].reshape(by_chip), moved[depth : 2 * depth].reshape(by_chip), 2
-        )
-        final_up = in_order(half, near, away, 3).reshape(depth, tall).astype(WIDE)
-        final_down = in_order(half, own_down, moved[2 * depth :], 0)
-        final_down = final_down.reshape(units, width).astype(WIDE)
-
+        own_down = share_three.astype(SHORT)
+        moved_down = swap_seq(own_down)
+        moved = swap_seq(jnp.concatenate([own, other], axis=0))
+        pair_two = own, other, moved
         split = share_one[: 2 * depth].reshape(2, depth, side).astype(SHORT)
         lines = share_one[2 * depth :, : 2 * LANES].reshape(LINES, 2, LANES)
         packet = jnp.pad(pick(lines, 1 - core, 1).astype(SHORT), ((0, 0), (0, side - LANES)))
@@ -685,7 +728,18 @@
             [line.astype(SHORT), share_one[2 * depth :, 2 * LANES :].astype(SHORT)], axis=1
         )
         packet = jnp.pad(packet, ((0, 0), (0, LANES)))
-        moved = swap_seq(jnp.concatenate([own, other[:depth], packet], axis=0))
+        packet = jnp.concatenate([own, other[:depth], packet], axis=0)
+        own_two, other_two, moved_two = after(packet, *pair_two)
+        moved = swap_seq(packet)
+        by_chip = (depth, chips, units // 2)
+        near = in_order(core, own_two.reshape(by_chip), other_two.reshape(by_chip), 2)
+        away = in_order(
+            core, moved_two[:depth].reshape(by_chip), moved_two[depth : 2 * depth].reshape(by_chip), 2
+        )
+        final_up = in_order(half, near, away, 3).reshape(depth, tall).astype(WIDE)
+        final_down = in_order(half, own_down, moved_down, 0)
+        final_down = final_down.reshape(units, width).astype(WIDE)
+
         by_third = (depth, 3, quarter)
         near = in_order(
             core,

time: 284 us -> 240 us (0.85)
  waiting for transfers between devices: 152 us -> 111 us
  starting transfers between devices: 42.1 us -> 67.3 us
  Pallas kernels: 54.6 us -> 30.2 us
    ppermute x8 -> x9, waiting for transfers between devices: 38.1 us -> 18.3 us  [gather_ring(): one = lax.ppermute(one, 'dp', far)]
    ppermute x14 -> x30, starting transfers between devices: 13.8 us -> 32.2 us  [the longest x12 15 us: sum_ring(): one = lax.ppermute(one, 'dp', far)]
    ppermute x10 -> x11, waiting for transfers between devices: 45.9 us -> 31.1 us  [swap_seq(): return lax.ppermute(array, 'seq', [(0, 1), (1, 0)])]
    ppermute x14 -> x30, waiting for transfers between devices: 45.4 us -> 37.8 us  [the longest x12 21 us: sum_ring(): one = lax.ppermute(one, 'dp', far)]
    ppermute x6 -> x9, waiting for transfers between devices: 13.9 us -> 20.4 us  [gather_ring(): two = lax.ppermute(two, 'dp', near)]
    pallas_call x1, Pallas kernels: 14.7 us -> 8.3 us  [per_device(): call(functools.partial(attention_back_kernel, micro, where_one), [((PARTS...]
    ppermute x17, waiting for transfers between devices: 8.79 us -> 2.99 us  [swap_core(): return lax.ppermute(array, 'dp', core_pairs)]
    concatenate x3 -> x8, other arithmetic: 0.1 us -> 3.92 us  [the longest x3 1.68 us: sum_ring(): one = jnp.concatenate([one + here[:cut], here[cut:]], axis=0)]
  transfers between devices with their start and end apart: 55 -> 76, of which waited for: 27 -> 41; matrix products, arithmetic and copies ran while one was open for 5% -> 7% of each run, Pallas kernels for 12% -> 5%
where the time goes in v1:
time: 240 us; the launch traced here: 239 us
  waiting for transfers between devices  111 us (46%)
  starting transfers between devices  67.3 us (28%)
  Pallas kernels  30.2 us (13%)
  local copies, waits for them, and re-layouts  17.5 us (7%)
  other arithmetic  12.2 us (5%)
    ppermute x11, waiting for transfers between devices, swap_seq(): return lax.ppermute(array, 'seq', [(0, 1), (1, 0)])  31.1 us
    ppermute x12, waiting for transfers between devices, sum_ring(): one = lax.ppermute(one, 'dp', far)  21 us
    ppermute x9, waiting for transfers between devices, gather_ring(): two = lax.ppermute(two, 'dp', near)  20.4 us
    ppermute x9, waiting for transfers between devices, gather_ring(): one = lax.ppermute(one, 'dp', far)  18.3 us
    ppermute x12, starting transfers between devices, sum_ring(): one = lax.ppermute(one, 'dp', far)  15 us
    ppermute x11, starting transfers between devices, swap_seq(): return lax.ppermute(array, 'seq', [(0, 1), (1, 0)])  13.2 us
    ppermute x9, starting transfers between devices, gather_ring(): one = lax.ppermute(one, 'dp', far)  10.5 us
    ppermute x12, starting transfers between devices, sum_ring(): two = lax.ppermute(two, 'dp', near)  10.4 us
  transfers between devices with their start and end apart: 76, of which 41 were waited for; matrix products, arithmetic and copies ran while one was open for 7% of the time, Pallas kernels for 5%

profile of v1, /device:TPU:0, one launch (start us, length us, event | category | flops | bytes accessed | tf_op | source)
XLA Modules:
  0.0 239.2 jit_solution(901853093480677988)
XLA Ops:
  7.6 3.0 %collective-permute-start.5 = (bf16[144,1280]{1,0:T(8,128)(2,1)S(1)}, bf16[144,1280]{1,0:T(8,128)(2,1)S(1)}, u32[]{:S(2)}, u32[]{:S(2)}) collective-permute-start(bf16[144,1280]{1,0:T(8,128)(2,1)S(1)} %fusion.18.refs_4_), channel_id=1, source_target_pairs={{0,4},{2,6},{8,0},{10,2},{16,8},{18,10},{24,16},{26,18},{28,24},{3... | collective-permute-start | bytes 1105928 | tf_op jit(solution)/shard_map/ppermute | solution.py:436
  10.8 8.7 %collective-permute-done.5.refs_6_ = bf16[144,1280]{1,0:T(8,128)(2,1)S(1)} collective-permute-done((bf16[144,1280]{1,0:T(8,128)(2,1)S(1)}, bf16[144,1280]{1,0:T(8,128)(2,1)S(1)}, u32[]{:S(2)}, u32[]{:S(2)}) %collective-permute-start.5) | collective-permute-done | bytes 368672 | tf_op jit(solution)/shard_map/ppermute | solution.py:436
  24.4 5.1 %collective-permute-done.refs_1_ = bf16[128,1024]{1,0:T(8,128)(2,1)S(1)} collective-permute-done((bf16[128,1024]{1,0:T(8,128)(2,1)S(1)}, bf16[128,1024]{1,0:T(8,128)(2,1)S(1)}, u32[]{:S(2)}, u32[]{:S(2)}) %collective-permute-start) | collective-permute-done | bytes 262176 | tf_op jit(solution)/shard_map/ppermute | solution.py:426
  33.3 6.1 %collective-permute-done.10.refs_10_ = bf16[144,1280]{1,0:T(8,128)(2,1)S(1)} collective-permute-done((bf16[144,1280]{1,0:T(8,128)(2,1)S(1)}, bf16[144,1280]{1,0:T(8,128)(2,1)S(1)}, u32[]{:S(2)}, u32[]{:S(2)}) %collective-permute-start.10) | collective-permute-done | bytes 368672 | tf_op jit(solution)/shard_map/ppermute | solution.py:436
  41.7 4.6 %collective-permute-done.11.refs_11_ = bf16[64,1280]{1,0:T(8,128)(2,1)S(1)} collective-permute-done((bf16[64,1280]{1,0:T(8,128)(2,1)S(1)}, bf16[64,1280]{1,0:T(8,128)(2,1)S(1)}, u32[]{:S(2)}, u32[]{:S(2)}) %collective-permute-start.11) | collective-permute-done | bytes 163872 | tf_op jit(solution)/shard_map/ppermute | solution.py:439
  46.2 6.1 %shard_map.263 = (bf16[512,1024]{1,0:T(8,128)(2,1)S(1)}, bf16[1024,768]{1,0:T(8,128)(2,1)S(1)}, bf16[512,768]{1,0:T(8,128)(2,1)S(1)}, bf16[256,256]{1,0:T(8,128)...) custom-call(bf16[128,1024]{1,0:T(8,128)(2,1)S(1)} %bitcast.216, ...), custom_call_target="tpu_custom_call" | custom-call | flops 1073741824 | bytes 8000000 | tf_op jit(solution)/shard_map/pallas_call | solution.py:561
  60.1 3.9 %collective-permute-done.20.refs_6_ = bf16[128,1024]{1,0:T(8,128)(2,1)S(1)} collective-permute-done((bf16[128,1024]{1,0:T(8,128)(2,1)S(1)}, bf16[128,1024]{1,0:T(8,128)(2,1)S(1)}, u32[]{:S(2)}, u32[]{:S(2)}) %collective-permute-start.20) | collective-permute-done | bytes 262176 | tf_op jit(solution)/shard_map/ppermute | solution.py:436
  69.7 3.6 %collective-permute-done.27.refs_14_ = bf16[128,1024]{1,0:T(8,128)(2,1)S(1)} collective-permute-done((bf16[128,1024]{1,0:T(8,128)(2,1)S(1)}, bf16[128,1024]{1,0:T(8,128)(2,1)S(1)}, u32[]{:S(2)}, u32[]{:S(2)}) %collective-permute-start.27) | collective-permute-done | bytes 262176 | tf_op jit(solution)/shard_map/ppermute | solution.py:435
  75.3 3.6 %collective-permute-done.21.refs_7_ = bf16[128,1024]{1,0:T(8,128)(2,1)S(1)} collective-permute-done((bf16[128,1024]{1,0:T(8,128)(2,1)S(1)}, bf16[128,1024]{1,0:T(8,128)(2,1)S(1)}, u32[]{:S(2)}, u32[]{:S(2)}) %collective-permute-start.21) | collective-permute-done | bytes 262176 | tf_op jit(solution)/shard_map/ppermute | solution.py:435
  80.9 3.6 %collective-permute-done.29.refs_16_ = bf16[128,1024]{1,0:T(8,128)(2,1)S(1)} collective-permute-done((bf16[128,1024]{1,0:T(8,128)(2,1)S(1)}, bf16[128,1024]{1,0:T(8,128)(2,1)S(1)}, u32[]{:S(2)}, u32[]{:S(2)}) %collective-permute-start.29) | collective-permute-done | bytes 262176 | tf_op jit(solution)/shard_map/ppermute | solution.py:435
  86.6 3.6 %collective-permute-done.23.refs_9_ = bf16[128,1024]{1,0:T(8,128)(2,1)S(1)} collective-permute-done((bf16[128,1024]{1,0:T(8,128)(2,1)S(1)}, bf16[128,1024]{1,0:T(8,128)(2,1)S(1)}, u32[]{:S(2)}, u32[]{:S(2)}) %collective-permute-start.23) | collective-permute-done | bytes 262176 | tf_op jit(solution)/shard_map/ppermute | solution.py:435
  96.5 2.8 %collective-permute-done.26.refs_12_ = bf16[64,1024]{1,0:T(8,128)(2,1)S(1)} collective-permute-done((bf16[64,1024]{1,0:T(8,128)(2,1)S(1)}, bf16[64,1024]{1,0:T(8,128)(2,1)S(1)}, u32[]{:S(2)}, u32[]{:S(2)}) %collective-permute-start.26) | collective-permute-done | bytes 131104 | tf_op jit(solution)/shard_map/ppermute | solution.py:439
  100.8 2.8 %shard_map.265 = (bf16[512,1024]{1,0:T(8,128)(2,1)S(1)}, bf16[1024,1024]{1,0:T(8,128)(2,1)S(1)}, bf16[1024,1024]{1,0:T(8,128)(2,1)S(1)}, f32[512,1024]{1,0:T(8,1...) custom-call(bf16[128,1024]{1,0:T(8,128)(2,1)S(1)} %get-tuple-element.98.refs_, ...), custom_call_target="tpu_custom_call" | custom-call | flops 2147483648 | bytes 16000000 | tf_op jit(solution)/shard_map/pallas_call | solution.py:601
  107.0 7.1 %collective-permute-done.36.from_seq = bf16[128,1024]{1,0:T(8,128)(2,1)S(1)} collective-permute-done((bf16[128,1024]{1,0:T(8,128)(2,1)S(1)}, bf16[128,1024]{1,0:T(8,128)(2,1)S(1)}, u32[]{:S(2)}, u32[]{:S(2)}) %collective-permute-start.36) | collective-permute-done | bytes 262176 | tf_op jit(solution)/shard_map/ppermute | solution.py:426
  116.5 6.3 %collective-permute-done.37.refs_1_ = bf16[128,1024]{1,0:T(8,128)(2,1)S(1)} collective-permute-done((bf16[128,1024]{1,0:T(8,128)(2,1)S(1)}, bf16[128,1024]{1,0:T(8,128)(2,1)S(1)}, u32[]{:S(2)}, u32[]{:S(2)}) %collective-permute-start.37) | collective-permute-done | bytes 262176 | tf_op jit(solution)/shard_map/ppermute | solution.py:426
  124.3 4.7 %shard_map.268 = (bf16[8,128,1024]{2,1,0:T(8,128)(2,1)S(1)}, bf16[8,128,1024]{2,1,0:T(8,128)(2,1)S(1)}, f32[2,128,1024]{2,1,0:T(8,128)S(1)}, bf16[2,128,1024]{2,1,0:T(8,128)(2,1)S(1)}, f32[1,1024]{1,0:T(1,128)S(1)}) custom-call(bf16[128,1024]{1,0:T(8,128)(2,1)S(1)} %get-tuple-element.115.refs_0_, bf16[128,1024]{1,0:T(8,128)(2,1)S(1)} %collective-permute-done.37.refs_1_, ...), custom_call_target="tpu_custom_call" | custom-call | flops 4294967296 | bytes 16000000 | tf_op jit(solution)/shard_map/pallas_call | solution.py:630
  136.5 3.0 %collective-permute-done.41.from_seq = bf16[128,1024]{1,0:T(8,128)(2,1)S(1)} collective-permute-done((bf16[128,1024]{1,0:T(8,128)(2,1)S(1)}, bf16[128,1024]{1,0:T(8,128)(2,1)S(1)}, u32[]{:S(2)}, u32[]{:S(2)}) %collective-permute-start.41) | collective-permute-done | bytes 262176 | tf_op jit(solution)/shard_map/ppermute | solution.py:426
  157.8 8.3 %shard_map.270 = (bf16[8,144,1280]{2,1,0:T(8,128)(2,1)S(1)}, bf16[512,768]{1,0:T(8,128)(2,1)S(1)}, f32[8,128]{1,0:T(8,128)}) custom-call(bf16[512,768]{1,0:T(8,128)(2,1)S(1)} %copy-done.12, f32[16,128,128]{2,1,0:T(8,128)S(1)} %copy-done.9, bf16[128,512]{1,0:T(8,128)(2,1)S(1)} %get-tuple-element.128.refs_2_, ...), custom_call_target="tpu_custom_call" | custom-call | flops 1610612736 | bytes 12000000 | tf_op jit(solution)/shard_map/pallas_call | solution.py:656
  189.2 2.8 %collective-permute-done.62 = bf16[128,1024]{1,0:T(8,128)(2,1)S(1)} collective-permute-done((bf16[128,1024]{1,0:T(8,128)(2,1)S(1)}, bf16[128,1024]{1,0:T(8,128)(2,1)S(1)}, u32[]{:S(2)}, u32[]{:S(2)}) %collective-permute-start.62) | collective-permute-done | bytes 262176 | tf_op jit(solution)/shard_map/ppermute | solution.py:458
  194.1 3.4 %collective-permute-done.72 = bf16[128,1024]{1,0:T(8,128)(2,1)S(1)} collective-permute-done((bf16[128,1024]{1,0:T(8,128)(2,1)S(1)}, bf16[128,1024]{1,0:T(8,128)(2,1)S(1)}, u32[]{:S(2)}, u32[]{:S(2)}) %collective-permute-start.72) | collective-permute-done | bytes 262176 | tf_op jit(solution)/shard_map/ppermute | solution.py:458
  200.2 3.0 %collective-permute-done.50 = bf16[144,1280]{1,0:T(8,128)(2,1)S(1)} collective-permute-done((bf16[144,1280]{1,0:T(8,128)(2,1)S(1)}, bf16[144,1280]{1,0:T(8,128)(2,1)S(1)}, u32[]{:S(2)}, u32[]{:S(2)}) %collective-permute-start.50) | collective-permute-done | bytes 368672 | tf_op jit(solution)/shard_map/ppermute | solution.py:447
  207.8 3.9 %collective-permute-done.51 = bf16[144,1280]{1,0:T(8,128)(2,1)S(1)} collective-permute-done((bf16[144,1280]{1,0:T(8,128)(2,1)S(1)}, bf16[144,1280]{1,0:T(8,128)(2,1)S(1)}, u32[]{:S(2)}, u32[]{:S(2)}) %collective-permute-start.51) | collective-permute-done | bytes 368672 | tf_op jit(solution)/shard_map/ppermute | solution.py:446
  216.0 4.5 %collective-permute-done.52 = bf16[144,1280]{1,0:T(8,128)(2,1)S(1)} collective-permute-done((bf16[144,1280]{1,0:T(8,128)(2,1)S(1)}, bf16[144,1280]{1,0:T(8,128)(2,1)S(1)}, u32[]{:S(2)}, u32[]{:S(2)}) %collective-permute-start.52) | collective-permute-done | bytes 368672 | tf_op jit(solution)/shard_map/ppermute | solution.py:458
  229.2 5.5 %collective-permute-done.56 = bf16[144,1280]{1,0:T(8,128)(2,1)S(1)} collective-permute-done((bf16[144,1280]{1,0:T(8,128)(2,1)S(1)}, bf16[144,1280]{1,0:T(8,128)(2,1)S(1)}, u32[]{:S(2)}, u32[]{:S(2)}) %collective-permute-start.56) | collective-permute-done | bytes 368672 | tf_op jit(solution)/shard_map/ppermute | solution.py:426
  (283 shorter events, 127.7 us)
Async XLA Ops:
  7.6 11.9 %collective-permute-start.5 = (bf16[144,1280]{1,0:T(8,128)(2,1)S(1)}, bf16[144,1280]{1,0:T(8,128)(2,1)S(1)}, u32[]{:S(2)}, u32[]{:S(2)}) collective-permute-start(bf16[144,1280]{1,0:T(8,128)(2,1)S(1)} %fusion.18.refs_4_), channel_id=1, source_target_pairs={{0,4},{2,6},{8,0},{10,2},{16,8},{18,10},{24,16},{26,18},{28,24},{3... | collective-permute-start | bytes 1105928 | tf_op jit(solution)/shard_map/ppermute | solution.py:436
  10.6 10.3 %collective-permute-start.4 = (bf16[144,1280]{1,0:T(8,128)(2,1)S(1)}, bf16[144,1280]{1,0:T(8,128)(2,1)S(1)}, u32[]{:S(2)}, u32[]{:S(2)}) collective-permute-start(bf16[144,1280]{1,0:T(8,128)(2,1)S(1)} %fusion.18.refs_4_), channel_id=1, source_target_pairs={{0,8},{2,10},{8,16},{10,18},{16,24},{18,26},{24,28},{26,30},{28,20... | collective-permute-start | bytes 1105928 | tf_op jit(solution)/shard_map/ppermute | solution.py:435
  53.3 14.3 %collective-permute-start.15 = (bf16[1024,512]{1,0:T(8,128)(2,1)S(1)}, bf16[1024,512]{1,0:T(8,128)(2,1)S(1)}, u32[]{:S(2)}, u32[]{:S(2)}) collective-permute-start(bf16[1024,512]{1,0:T(8,128)(2,1)S(1)} %get-tuple-element.95.mine), channel_id=1, source_target_pairs={{0,2},{2,0},{4,6},{6,4},{8,10},{10,8},{12,14},{14,12},{16,18},{18,... | collective-permute-start | bytes 3145736 | tf_op jit(solution)/shard_map/ppermute | solution.py:423
  59.3 10.3 %collective-permute-start.28 = (bf16[128,1024]{1,0:T(8,128)(2,1)S(1)}, bf16[128,1024]{1,0:T(8,128)(2,1)S(1)}, u32[]{:S(2)}, u32[]{:S(2)}) collective-permute-start(bf16[128,1024]{1,0:T(8,128)(2,1)S(1)} %dynamic-slice_bitcast_fusion.refs_13_), channel_id=1, source_target_pairs={{0,8},{2,10},{8,16},{10,18},{16,24},{18,26},{24,28},{26,30},{28,20... | collective-permute-start | bytes 786440 | tf_op jit(solution)/shard_map/ppermute | solution.py:436
  65.6 13.3 %collective-permute-start.21 = (bf16[128,1024]{1,0:T(8,128)(2,1)S(1)}, bf16[128,1024]{1,0:T(8,128)(2,1)S(1)}, u32[]{:S(2)}, u32[]{:S(2)}) collective-permute-start(bf16[128,1024]{1,0:T(8,128)(2,1)S(1)} %collective-permute-done.19.refs_5_), channel_id=1, source_target_pairs={{0,4},{2,6},{8,0},{10,2},{16,8},{18,10},{24,16},{26,18},{28,24},{3... | collective-permute-start | bytes 786440 | tf_op jit(solution)/shard_map/ppermute | solution.py:435
  67.2 11.7 %collective-permute-start.22 = (bf16[128,1024]{1,0:T(8,128)(2,1)S(1)}, bf16[128,1024]{1,0:T(8,128)(2,1)S(1)}, u32[]{:S(2)}, u32[]{:S(2)}) collective-permute-start(bf16[128,1024]{1,0:T(8,128)(2,1)S(1)} %collective-permute-done.20.refs_6_), channel_id=1, source_target_pairs={{0,8},{2,10},{8,16},{10,18},{16,24},{18,26},{24,28},{26,30},{28,20... | collective-permute-start | bytes 786440 | tf_op jit(solution)/shard_map/ppermute | solution.py:436
  68.4 10.5 %collective-permute-start.16 = (bf16[128,1024]{1,0:T(8,128)(2,1)S(1)}, bf16[128,1024]{1,0:T(8,128)(2,1)S(1)}, u32[]{:S(2)}, u32[]{:S(2)}) collective-permute-start(bf16[128,1024]{1,0:T(8,128)(2,1)S(1)} %get-tuple-element.98.refs_0_), channel_id=1, source_target_pairs={{0,1},{1,0},{2,3},{3,2},{4,5},{5,4},{6,7},{7,6},{8,9},{9,8},{10,11... | collective-permute-start | bytes 786440 | tf_op jit(solution)/shard_map/ppermute | solution.py:426
  73.3 11.2 %collective-permute-start.29 = (bf16[128,1024]{1,0:T(8,128)(2,1)S(1)}, bf16[128,1024]{1,0:T(8,128)(2,1)S(1)}, u32[]{:S(2)}, u32[]{:S(2)}) collective-permute-start(bf16[128,1024]{1,0:T(8,128)(2,1)S(1)} %collective-permute-done.27.refs_14_), channel_id=1, source_target_pairs={{0,4},{2,6},{8,0},{10,2},{16,8},{18,10},{24,16},{26,18},{28,24},{3... | collective-permute-start | bytes 786440 | tf_op jit(solution)/shard_map/ppermute | solution.py:435
  78.9 11.2 %collective-permute-start.23 = (bf16[128,1024]{1,0:T(8,128)(2,1)S(1)}, bf16[128,1024]{1,0:T(8,128)(2,1)S(1)}, u32[]{:S(2)}, u32[]{:S(2)}) collective-permute-start(bf16[128,1024]{1,0:T(8,128)(2,1)S(1)} %collective-permute-done.21.refs_7_), channel_id=1, source_target_pairs={{0,4},{2,6},{8,0},{10,2},{16,8},{18,10},{24,16},{26,18},{28,24},{3... | collective-permute-start | bytes 786440 | tf_op jit(solution)/shard_map/ppermute | solution.py:435
  143.7 22.3 %collective-permute-start.69 = (bf16[128,1024]{1,0:T(8,128)(2,1)}, bf16[128,1024]{1,0:T(8,128)(2,1)}, u32[]{:S(2)}, u32[]{:S(2)}) collective-permute-start(bf16[128,1024]{1,0:T(8,128)(2,1)} %pad_maximum_fusion.9), channel_id=1, source_target_pairs={{0,8},{2,10},{8,16},{10,18},{16,24},{18,26},{24,28},{26,30},{28,20... | collective-permute-start | bytes 786440 | tf_op jit(solution)/shard_map/ppermute | solution.py:446
  145.2 20.9 %collective-permute-start.59 = (bf16[128,1024]{1,0:T(8,128)(2,1)}, bf16[128,1024]{1,0:T(8,128)(2,1)}, u32[]{:S(2)}, u32[]{:S(2)}) collective-permute-start(bf16[128,1024]{1,0:T(8,128)(2,1)} %pad_maximum_fusion.6), channel_id=1, source_target_pairs={{0,8},{2,10},{8,16},{10,18},{16,24},{18,26},{24,28},{26,30},{28,20... | collective-permute-start | bytes 786440 | tf_op jit(solution)/shard_map/ppermute | solution.py:446
  148.8 17.3 %collective-permute-start.70 = (bf16[128,1024]{1,0:T(8,128)(2,1)}, bf16[128,1024]{1,0:T(8,128)(2,1)}, u32[]{:S(2)}, u32[]{:S(2)}) collective-permute-start(bf16[128,1024]{1,0:T(8,128)(2,1)} %pad_maximum_fusion.10), channel_id=1, source_target_pairs={{0,4},{2,6},{8,0},{10,2},{16,8},{18,10},{24,16},{26,18},{28,24},{3... | collective-permute-start | bytes 786440 | tf_op jit(solution)/shard_map/ppermute | solution.py:447
  151.8 14.3 %collective-permute-start.60 = (bf16[128,1024]{1,0:T(8,128)(2,1)}, bf16[128,1024]{1,0:T(8,128)(2,1)}, u32[]{:S(2)}, u32[]{:S(2)}) collective-permute-start(bf16[128,1024]{1,0:T(8,128)(2,1)} %pad_maximum_fusion.7), channel_id=1, source_target_pairs={{0,4},{2,6},{8,0},{10,2},{16,8},{18,10},{24,16},{26,18},{28,24},{3... | collective-permute-start | bytes 786440 | tf_op jit(solution)/shard_map/ppermute | solution.py:447
  170.7 10.2 %collective-permute-start.71 = (bf16[128,1024]{1,0:T(8,128)(2,1)S(1)}, bf16[128,1024]{1,0:T(8,128)(2,1)S(1)}, u32[]{:S(2)}, u32[]{:S(2)}) collective-permute-start(bf16[128,1024]{1,0:T(8,128)(2,1)S(1)} %get-tuple-element.173), channel_id=1, source_target_pairs={{0,8},{2,10},{8,16},{10,18},{16,24},{18,26},{24,28},{26,30},{28,20... | collective-permute-start | bytes 786440 | tf_op jit(solution)/shard_map/ppermute | solution.py:446
  172.3 11.6 %collective-permute-start.73 = (bf16[128,1024]{1,0:T(8,128)(2,1)S(1)}, bf16[128,1024]{1,0:T(8,128)(2,1)S(1)}, u32[]{:S(2)}, u32[]{:S(2)}) collective-permute-start(bf16[128,1024]{1,0:T(8,128)(2,1)S(1)} %get-tuple-element.174), channel_id=1, source_target_pairs={{0,4},{2,6},{8,0},{10,2},{16,8},{18,10},{24,16},{26,18},{28,24},{3... | collective-permute-start | bytes 786440 | tf_op jit(solution)/shard_map/ppermute | solution.py:447
  173.9 10.5 %collective-permute-start.45 = (bf16[2,128,1024]{2,1,0:T(8,128)(2,1)S(1)}, bf16[2,128,1024]{2,1,0:T(8,128)(2,1)S(1)}, u32[]{:S(2)}, u32[]{:S(2)}) collective-permute-start(bf16[2,128,1024]{2,1,0:T(8,128)(2,1)S(1)} %get-tuple-element.139), channel_id=1, source_target_pairs={{0,2},{2,0},{4,6},{6,4},{8,10},{10,8},{12,14},{14,12},{16,18},{18,... | collective-permute-start | bytes 1572872 | tf_op jit(solution)/shard_map/ppermute | solution.py:423
  176.7 10.7 %collective-permute-start.47 = (bf16[64,1280]{1,0:T(8,128)(2,1)S(1)}, bf16[64,1280]{1,0:T(8,128)(2,1)S(1)}, u32[]{:S(2)}, u32[]{:S(2)}) collective-permute-start(bf16[64,1280]{1,0:T(8,128)(2,1)S(1)} %get-tuple-element.168), channel_id=1, source_target_pairs={{0,4},{2,6},{8,0},{10,2},{16,8},{18,10},{24,16},{26,18},{28,24},{3... | collective-permute-start | bytes 491528 | tf_op jit(solution)/shard_map/ppermute | solution.py:446
  180.9 11.0 %collective-permute-start.62 = (bf16[128,1024]{1,0:T(8,128)(2,1)S(1)}, bf16[128,1024]{1,0:T(8,128)(2,1)S(1)}, u32[]{:S(2)}, u32[]{:S(2)}) collective-permute-start(bf16[128,1024]{1,0:T(8,128)(2,1)S(1)} %get-tuple-element.181), channel_id=1, source_target_pairs={{0,8},{2,10},{8,16},{10,18},{16,24},{18,26},{24,28},{26,30},{28,20... | collective-permute-start | bytes 786440 | tf_op jit(solution)/shard_map/ppermute | solution.py:458
  184.3 13.2 %collective-permute-start.72 = (bf16[128,1024]{1,0:T(8,128)(2,1)S(1)}, bf16[128,1024]{1,0:T(8,128)(2,1)S(1)}, u32[]{:S(2)}, u32[]{:S(2)}) collective-permute-start(bf16[128,1024]{1,0:T(8,128)(2,1)S(1)} %get-tuple-element.171), channel_id=1, source_target_pairs={{0,8},{2,10},{8,16},{10,18},{16,24},{18,26},{24,28},{26,30},{28,20... | collective-permute-start | bytes 786440 | tf_op jit(solution)/shard_map/ppermute | solution.py:458
  187.4 11.3 %collective-permute-start.74 = (bf16[128,1024]{1,0:T(8,128)(2,1)S(1)}, bf16[128,1024]{1,0:T(8,128)(2,1)S(1)}, u32[]{:S(2)}, u32[]{:S(2)}) collective-permute-start(bf16[128,1024]{1,0:T(8,128)(2,1)S(1)} %get-tuple-element.172), channel_id=1, source_target_pairs={{0,4},{2,6},{8,0},{10,2},{16,8},{18,10},{24,16},{26,18},{28,24},{3... | collective-permute-start | bytes 786440 | tf_op jit(solution)/shard_map/ppermute | solution.py:459
  187.7 12.5 %collective-permute-start.46 = (bf16[128,1024]{1,0:T(8,128)(2,1)S(1)}, bf16[128,1024]{1,0:T(8,128)(2,1)S(1)}, u32[]{:S(2)}, u32[]{:S(2)}) collective-permute-start(bf16[128,1024]{1,0:T(8,128)(2,1)S(1)} %fusion.22), channel_id=1, source_target_pairs={{0,1},{1,0},{2,3},{3,2},{4,5},{5,4},{6,7},{7,6},{8,9},{9,8},{10,11... | collective-permute-start | bytes 786440 | tf_op jit(solution)/shard_map/ppermute | solution.py:426
  191.9 11.2 %collective-permute-start.50 = (bf16[144,1280]{1,0:T(8,128)(2,1)S(1)}, bf16[144,1280]{1,0:T(8,128)(2,1)S(1)}, u32[]{:S(2)}, u32[]{:S(2)}) collective-permute-start(bf16[144,1280]{1,0:T(8,128)(2,1)S(1)} %pad_maximum_fusion.2), channel_id=1, source_target_pairs={{0,8},{2,10},{8,16},{10,18},{16,24},{18,26},{24,28},{26,30},{28,20... | collective-permute-start | bytes 1105928 | tf_op jit(solution)/shard_map/ppermute | solution.py:447
  206.5 18.7 %collective-permute-start.66 = (bf16[128,1024]{1,0:T(8,128)(2,1)}, bf16[128,1024]{1,0:T(8,128)(2,1)}, u32[]{:S(2)}, u32[]{:S(2)}) collective-permute-start(bf16[128,1024]{1,0:T(8,128)(2,1)} %pad_maximum_fusion.8), channel_id=1, source_target_pairs={{0,1},{1,0},{2,3},{3,2},{4,5},{5,4},{6,7},{7,6},{8,9},{9,8},{10,11... | collective-permute-start | bytes 786440 | tf_op jit(solution)/shard_map/ppermute | solution.py:426
  223.9 10.8 %collective-permute-start.56 = (bf16[144,1280]{1,0:T(8,128)(2,1)S(1)}, bf16[144,1280]{1,0:T(8,128)(2,1)S(1)}, u32[]{:S(2)}, u32[]{:S(2)}) collective-permute-start(bf16[144,1280]{1,0:T(8,128)(2,1)S(1)} %pad_maximum_fusion.3), channel_id=1, source_target_pairs={{0,1},{1,0},{2,3},{3,2},{4,5},{5,4},{6,7},{7,6},{8,9},{9,8},{10,11... | collective-permute-start | bytes 1105928 | tf_op jit(solution)/shard_map/ppermute | solution.py:426
  (73 other events, 619.2 us)

commit v2 on v1

--- a/solution.py
+++ b/solution.py
@@ -13,7 +13,7 @@
 PARTS = 8
 SHORT = jnp.bfloat16
 WIDE = jnp.float32
-LIMIT = 24 * 1024 * 1024
+LIMIT = 12 * 1024 * 1024
 WHOLE = 56 * 1024 * 1024
 LINES = 16
 LANES = 256
@@ -326,7 +326,7 @@
     left, right = short[:, : width // 2], short[:, width // 2 :]
     own = jnp.where(core == 0, left, right)
     away = jnp.where(core == 0, right, left)
-    out_keep[...] = inner_rows(context[...], own)
+    out_keep[...] = inner_rows(context[...], own).astype(SHORT)
     out_send[...] = inner_rows(context[...], away).astype(SHORT)
     for target, which in ((ctx_keep, core), (ctx_send, 1 - core)):
         for side, which_half in enumerate((half, 1 - half)):
@@ -379,7 +379,7 @@
         spot = block(where(step, chip), 128)
         chunks[step, :128, : 3 * quarter] = inner_rows(tokens[:, spot], grad[...]).astype(SHORT)
         chunks[step, :128, 3 * quarter :] = (
-            out_keep[spot, :] + out_core[spot, :].astype(WIDE)
+            out_keep[spot, :].astype(WIDE) + out_core[spot, :].astype(WIDE)
         ).astype(SHORT)
         lines = vectors[:, spot].astype(SHORT)
         chunks[step, 128:, :] = jnp.zeros((LINES, chunks.shape[2]), SHORT)
@@ -393,6 +393,27 @@
     for side in range(2):
         out = times_back(grad[side * tall : (side + 1) * tall, :], full[...])
         split_rows(out, side * tall, micro, rows, keep, send)
+
+
+def final_kernel(own, other, moved, line, grad_qkv, grad_out, total):
+    _, core, half = here()
+    depth, width = grad_out.shape
+    quarter = width // 4
+    flip_core, flip_half = 1 - core, 1 - half
+    sources = (
+        (own[...], half, core),
+        (other[:depth, :], half, flip_core),
+        (moved[:depth, :], flip_half, core),
+        (moved[depth : 2 * depth, :], flip_half, flip_core),
+    )
+    for value, side, which in sources:
+        for third in range(3):
+            spot = block(4 * third + 2 * side + which, quarter)
+            grad_qkv[:, spot] = value[:, third * quarter : (third + 1) * quarter].astype(WIDE)
+    parts = [value[:, 3 * quarter :].astype(WIDE) for value, _, _ in sources]
+    grad_out[:, block(core, width // 2)] = parts[0] + parts[2]
+    grad_out[:, block(flip_core, width // 2)] = parts[1] + parts[3]
+    total[...] = line[...] + moved[2 * depth :, :LANES].astype(WIDE)
 
 
 def after(gate, *values):
@@ -641,7 +662,7 @@
             first_back_kernel,
             [
                 ((own_rows, width), WIDE),
-                ((width, width // 2), WIDE),
+                ((width, width // 2), SHORT),
                 ((width, width // 2), SHORT),
                 ((own_rows, width // 2), SHORT),
                 ((own_rows, width // 2), SHORT),
@@ -690,7 +711,7 @@
 
         if ringed:
             share_three = sum_ring(grads_three, 64, True, (gate_one, flag, None))
-            share_two = sum_ring(grads_two, 64, True, (gate_one, flag, None))
+            share_two = sum_ring(grads_two, 64, True, (gate_one, grad_seq, flag))
             share_one = sum_ring(grads_one, 64, False, gates_one)
         else:
             whole = grads_three.reshape(chips, units // 2, width)
@@ -740,26 +761,11 @@
         final_down = in_order(half, own_down, moved_down, 0)
         final_down = final_down.reshape(units, width).astype(WIDE)
 
-        by_third = (depth, 3, quarter)
-        near = in_order(
-            core,
-            own[:, : 3 * quarter].reshape(by_third),
-            other[:depth, : 3 * quarter].reshape(by_third),
-            2,
-        )
-        away = in_order(
-            core,
-            moved[:depth, : 3 * quarter].reshape(by_third),
-            moved[depth : 2 * depth, : 3 * quarter].reshape(by_third),
-            2,
-        )
-        final_qkv = in_order(half, near, away, 2).reshape(depth, 3 * width).astype(WIDE)
-        near = own[:, 3 * quarter :].astype(WIDE) + moved[:depth, 3 * quarter :].astype(WIDE)
-        away = other[:depth, 3 * quarter :].astype(WIDE) + moved[
-            depth : 2 * depth, 3 * quarter :
-        ].astype(WIDE)
-        final_out = in_order(core, near, away, 1).reshape(depth, width)
-        line = line + moved[2 * depth :, :LANES].astype(WIDE)
+        final_qkv, final_out, line = call(
+            final_kernel,
+            [((depth, 3 * width), WIDE), ((depth, width), WIDE), ((LINES, LANES), WIDE)],
+            moved=2 * 10**6,
+        )(own, other, moved, line)
         finals = [line[i, :depth] for i in range(8)]
         from_seq = moved[2 * depth + 8, LANES : LANES + units // 2].astype(WIDE)
         final_bias = in_order(half, bias, from_seq, 0).reshape(-1)

time: 240 us -> 238 us (level)
  local copies, waits for them, and re-layouts: 17.5 us -> 14.7 us
    ppermute x12, waiting for transfers between devices: 21 us -> 18.5 us  [sum_ring(): one = lax.ppermute(one, 'dp', far)]
    ppermute x12, starting transfers between devices: 10.4 us -> 13 us  [sum_ring(): two = lax.ppermute(two, 'dp', near)]
    unnamed x52 -> x44, local copies, waits for them, and re-layouts: 6.65 us -> 6.93 us
  transfers between devices with their start and end apart: 76 -> 76, of which waited for: 41 -> 38; matrix products, arithmetic and copies ran while one was open for 7% -> 7% of each run, Pallas kernels for 5% -> 5%
where the time goes in v2:
time: 238 us; the launch traced here: 237 us
  waiting for transfers between devices  110 us (46%)
  starting transfers between devices  68.3 us (29%)
  Pallas kernels  31.1 us (13%)
  local copies, waits for them, and re-layouts  14.7 us (6%)
  other arithmetic  11.6 us (5%)
    ppermute x11, waiting for transfers between devices, swap_seq(): return lax.ppermute(array, 'seq', [(0, 1), (1, 0)])  33.2 us
    ppermute x9, waiting for transfers between devices, gather_ring(): two = lax.ppermute(two, 'dp', near)  20.4 us
    ppermute x12, waiting for transfers between devices, sum_ring(): one = lax.ppermute(one, 'dp', far)  18.5 us
    ppermute x9, waiting for transfers between devices, gather_ring(): one = lax.ppermute(one, 'dp', far)  18.3 us
    ppermute x11, starting transfers between devices, swap_seq(): return lax.ppermute(array, 'seq', [(0, 1), (1, 0)])  13.7 us
    ppermute x12, starting transfers between devices, sum_ring(): one = lax.ppermute(one, 'dp', far)  13.3 us
    ppermute x12, starting transfers between devices, sum_ring(): two = lax.ppermute(two, 'dp', near)  13 us
    ppermute x9, starting transfers between devices, gather_ring(): one = lax.ppermute(one, 'dp', far)  10.5 us
  transfers between devices with their start and end apart: 76, of which 38 were waited for; matrix products, arithmetic and copies ran while one was open for 7% of the time, Pallas kernels for 5%

profile of v2, /device:TPU:0, one launch (start us, length us, event | category | flops | bytes accessed | tf_op | source)
XLA Modules:
  0.0 237.2 jit_solution(84437003775205655)
XLA Ops:
  7.6 3.0 %collective-permute-start.5 = (bf16[144,1280]{1,0:T(8,128)(2,1)S(1)}, bf16[144,1280]{1,0:T(8,128)(2,1)S(1)}, u32[]{:S(2)}, u32[]{:S(2)}) collective-permute-start(bf16[144,1280]{1,0:T(8,128)(2,1)S(1)} %fusion.18.refs_4_), channel_id=1, source_target_pairs={{0,4},{2,6},{8,0},{10,2},{16,8},{18,10},{24,16},{26,18},{28,24},{3... | collective-permute-start | bytes 1105928 | tf_op jit(solution)/shard_map/ppermute | solution.py:457
  10.8 8.7 %collective-permute-done.5.refs_6_ = bf16[144,1280]{1,0:T(8,128)(2,1)S(1)} collective-permute-done((bf16[144,1280]{1,0:T(8,128)(2,1)S(1)}, bf16[144,1280]{1,0:T(8,128)(2,1)S(1)}, u32[]{:S(2)}, u32[]{:S(2)}) %collective-permute-start.5) | collective-permute-done | bytes 368672 | tf_op jit(solution)/shard_map/ppermute | solution.py:457
  24.4 5.1 %collective-permute-done.refs_1_ = bf16[128,1024]{1,0:T(8,128)(2,1)S(1)} collective-permute-done((bf16[128,1024]{1,0:T(8,128)(2,1)S(1)}, bf16[128,1024]{1,0:T(8,128)(2,1)S(1)}, u32[]{:S(2)}, u32[]{:S(2)}) %collective-permute-start) | collective-permute-done | bytes 262176 | tf_op jit(solution)/shard_map/ppermute | solution.py:447
  33.3 6.1 %collective-permute-done.10.refs_10_ = bf16[144,1280]{1,0:T(8,128)(2,1)S(1)} collective-permute-done((bf16[144,1280]{1,0:T(8,128)(2,1)S(1)}, bf16[144,1280]{1,0:T(8,128)(2,1)S(1)}, u32[]{:S(2)}, u32[]{:S(2)}) %collective-permute-start.10) | collective-permute-done | bytes 368672 | tf_op jit(solution)/shard_map/ppermute | solution.py:457
  41.7 4.6 %collective-permute-done.11.refs_11_ = bf16[64,1280]{1,0:T(8,128)(2,1)S(1)} collective-permute-done((bf16[64,1280]{1,0:T(8,128)(2,1)S(1)}, bf16[64,1280]{1,0:T(8,128)(2,1)S(1)}, u32[]{:S(2)}, u32[]{:S(2)}) %collective-permute-start.11) | collective-permute-done | bytes 163872 | tf_op jit(solution)/shard_map/ppermute | solution.py:460
  46.2 6.1 %shard_map.263 = (bf16[512,1024]{1,0:T(8,128)(2,1)S(1)}, bf16[1024,768]{1,0:T(8,128)(2,1)S(1)}, bf16[512,768]{1,0:T(8,128)(2,1)S(1)}, bf16[256,256]{1,0:T(8,128)...) custom-call(bf16[128,1024]{1,0:T(8,128)(2,1)S(1)} %bitcast.206, ...), custom_call_target="tpu_custom_call" | custom-call | flops 1073741824 | bytes 8000000 | tf_op jit(solution)/shard_map/pallas_call | solution.py:582
  61.1 3.9 %collective-permute-done.20.refs_6_ = bf16[128,1024]{1,0:T(8,128)(2,1)S(1)} collective-permute-done((bf16[128,1024]{1,0:T(8,128)(2,1)S(1)}, bf16[128,1024]{1,0:T(8,128)(2,1)S(1)}, u32[]{:S(2)}, u32[]{:S(2)}) %collective-permute-start.20) | collective-permute-done | bytes 262176 | tf_op jit(solution)/shard_map/ppermute | solution.py:457
  70.6 3.6 %collective-permute-done.27.refs_14_ = bf16[128,1024]{1,0:T(8,128)(2,1)S(1)} collective-permute-done((bf16[128,1024]{1,0:T(8,128)(2,1)S(1)}, bf16[128,1024]{1,0:T(8,128)(2,1)S(1)}, u32[]{:S(2)}, u32[]{:S(2)}) %collective-permute-start.27) | collective-permute-done | bytes 262176 | tf_op jit(solution)/shard_map/ppermute | solution.py:456
  76.3 3.6 %collective-permute-done.21.refs_7_ = bf16[128,1024]{1,0:T(8,128)(2,1)S(1)} collective-permute-done((bf16[128,1024]{1,0:T(8,128)(2,1)S(1)}, bf16[128,1024]{1,0:T(8,128)(2,1)S(1)}, u32[]{:S(2)}, u32[]{:S(2)}) %collective-permute-start.21) | collective-permute-done | bytes 262176 | tf_op jit(solution)/shard_map/ppermute | solution.py:456
  81.9 3.6 %collective-permute-done.29.refs_16_ = bf16[128,1024]{1,0:T(8,128)(2,1)S(1)} collective-permute-done((bf16[128,1024]{1,0:T(8,128)(2,1)S(1)}, bf16[128,1024]{1,0:T(8,128)(2,1)S(1)}, u32[]{:S(2)}, u32[]{:S(2)}) %collective-permute-start.29) | collective-permute-done | bytes 262176 | tf_op jit(solution)/shard_map/ppermute | solution.py:456
  87.5 3.6 %collective-permute-done.23.refs_9_ = bf16[128,1024]{1,0:T(8,128)(2,1)S(1)} collective-permute-done((bf16[128,1024]{1,0:T(8,128)(2,1)S(1)}, bf16[128,1024]{1,0:T(8,128)(2,1)S(1)}, u32[]{:S(2)}, u32[]{:S(2)}) %collective-permute-start.23) | collective-permute-done | bytes 262176 | tf_op jit(solution)/shard_map/ppermute | solution.py:456
  97.5 2.8 %collective-permute-done.26.refs_12_ = bf16[64,1024]{1,0:T(8,128)(2,1)S(1)} collective-permute-done((bf16[64,1024]{1,0:T(8,128)(2,1)S(1)}, bf16[64,1024]{1,0:T(8,128)(2,1)S(1)}, u32[]{:S(2)}, u32[]{:S(2)}) %collective-permute-start.26) | collective-permute-done | bytes 131104 | tf_op jit(solution)/shard_map/ppermute | solution.py:460
  101.8 2.8 %shard_map.265 = (bf16[512,1024]{1,0:T(8,128)(2,1)S(1)}, bf16[1024,1024]{1,0:T(8,128)(2,1)S(1)}, bf16[1024,1024]{1,0:T(8,128)(2,1)S(1)}, f32[512,1024]{1,0:T(8,1...) custom-call(bf16[128,1024]{1,0:T(8,128)(2,1)S(1)} %get-tuple-element.103.refs, ...), custom_call_target="tpu_custom_call" | custom-call | flops 2147483648 | bytes 16000000 | tf_op jit(solution)/shard_map/pallas_call | solution.py:622
  108.0 7.1 %collective-permute-done.36.from_seq = bf16[128,1024]{1,0:T(8,128)(2,1)S(1)} collective-permute-done((bf16[128,1024]{1,0:T(8,128)(2,1)S(1)}, bf16[128,1024]{1,0:T(8,128)(2,1)S(1)}, u32[]{:S(2)}, u32[]{:S(2)}) %collective-permute-start.36) | collective-permute-done | bytes 262176 | tf_op jit(solution)/shard_map/ppermute | solution.py:447
  117.4 6.3 %collective-permute-done.37.refs_1_ = bf16[128,1024]{1,0:T(8,128)(2,1)S(1)} collective-permute-done((bf16[128,1024]{1,0:T(8,128)(2,1)S(1)}, bf16[128,1024]{1,0:T(8,128)(2,1)S(1)}, u32[]{:S(2)}, u32[]{:S(2)}) %collective-permute-start.37) | collective-permute-done | bytes 262176 | tf_op jit(solution)/shard_map/ppermute | solution.py:447
  125.2 4.7 %shard_map.268 = (bf16[8,128,1024]{2,1,0:T(8,128)(2,1)S(1)}, bf16[8,128,1024]{2,1,0:T(8,128)(2,1)S(1)}, f32[2,128,1024]{2,1,0:T(8,128)S(1)}, bf16[2,128,1024]{2,1,0:T(8,128)(2,1)S(1)}, f32[1,1024]{1,0:T(1,128)S(1)}) custom-call(bf16[128,1024]{1,0:T(8,128)(2,1)S(1)} %get-tuple-element.120.refs_0_, bf16[128,1024]{1,0:T(8,128)(2,1)S(1)} %collective-permute-done.37.refs_1_, ...), custom_call_target="tpu_custom_call" | custom-call | flops 4294967296 | bytes 16000000 | tf_op jit(solution)/shard_map/pallas_call | solution.py:651
  137.4 3.0 %collective-permute-done.41.from_seq = bf16[128,1024]{1,0:T(8,128)(2,1)S(1)} collective-permute-done((bf16[128,1024]{1,0:T(8,128)(2,1)S(1)}, bf16[128,1024]{1,0:T(8,128)(2,1)S(1)}, u32[]{:S(2)}, u32[]{:S(2)}) %collective-permute-start.41) | collective-permute-done | bytes 262176 | tf_op jit(solution)/shard_map/ppermute | solution.py:447
  148.6 2.7 %collective-permute-done.43.refs_4_ = bf16[256,256]{1,0:T(8,128)(2,1)S(1)} collective-permute-done((bf16[256,256]{1,0:T(8,128)(2,1)S(1)}, bf16[256,256]{1,0:T(8,128)(2,1)S(1)}, u32[]{:S(2)}, u32[]{:S(2)}) %collective-permute-start.43) | collective-permute-done | bytes 131104 | tf_op jit(solution)/shard_map/ppermute | solution.py:447
  160.7 8.2 %shard_map.270 = (bf16[8,144,1280]{2,1,0:T(8,128)(2,1)S(1)}, bf16[512,768]{1,0:T(8,128)(2,1)S(1)}, f32[8,128]{1,0:T(8,128)}) custom-call(bf16[512,768]{1,0:T(8,128)(2,1)S(1)} %copy-done.14, f32[16,128,128]{2,1,0:T(8,128)S(1)} %copy-done.10, bf16[128,512]{1,0:T(8,128)(2,1)S(1)} %get-tuple-element.133.refs_2_, ...), custom_call_target="tpu_custom_call" | custom-call | flops 1610612736 | bytes 12000000 | tf_op jit(solution)/shard_map/pallas_call | solution.py:677
  176.9 6.3 %collective-permute-done.71 = bf16[128,1024]{1,0:T(8,128)(2,1)S(1)} collective-permute-done((bf16[128,1024]{1,0:T(8,128)(2,1)S(1)}, bf16[128,1024]{1,0:T(8,128)(2,1)S(1)}, u32[]{:S(2)}, u32[]{:S(2)}) %collective-permute-start.71) | collective-permute-done | bytes 262176 | tf_op jit(solution)/shard_map/ppermute | solution.py:467
  195.5 3.0 %collective-permute-done.72 = bf16[128,1024]{1,0:T(8,128)(2,1)S(1)} collective-permute-done((bf16[128,1024]{1,0:T(8,128)(2,1)S(1)}, bf16[128,1024]{1,0:T(8,128)(2,1)S(1)}, u32[]{:S(2)}, u32[]{:S(2)}) %collective-permute-start.72) | collective-permute-done | bytes 262176 | tf_op jit(solution)/shard_map/ppermute | solution.py:479
  207.9 3.2 %collective-permute-done.51 = bf16[144,1280]{1,0:T(8,128)(2,1)S(1)} collective-permute-done((bf16[144,1280]{1,0:T(8,128)(2,1)S(1)}, bf16[144,1280]{1,0:T(8,128)(2,1)S(1)}, u32[]{:S(2)}, u32[]{:S(2)}) %collective-permute-start.51) | collective-permute-done | bytes 368672 | tf_op jit(solution)/shard_map/ppermute | solution.py:467
  215.2 4.5 %collective-permute-done.52 = bf16[144,1280]{1,0:T(8,128)(2,1)S(1)} collective-permute-done((bf16[144,1280]{1,0:T(8,128)(2,1)S(1)}, bf16[144,1280]{1,0:T(8,128)(2,1)S(1)}, u32[]{:S(2)}, u32[]{:S(2)}) %collective-permute-start.52) | collective-permute-done | bytes 368672 | tf_op jit(solution)/shard_map/ppermute | solution.py:479
  229.7 5.3 %collective-permute-done.56.moved = bf16[144,1280]{1,0:T(8,128)(2,1)S(1)} collective-permute-done((bf16[144,1280]{1,0:T(8,128)(2,1)}, bf16[144,1280]{1,0:T(8,128)(2,1)S(1)}, u32[]{:S(2)}, u32[]{:S(2)}) %collective-permute-start.56) | collective-permute-done | bytes 368672 | tf_op jit(solution)/shard_map/ppermute | solution.py:447
  (261 shorter events, 124.0 us)
Async XLA Ops:
  7.6 11.9 %collective-permute-start.5 = (bf16[144,1280]{1,0:T(8,128)(2,1)S(1)}, bf16[144,1280]{1,0:T(8,128)(2,1)S(1)}, u32[]{:S(2)}, u32[]{:S(2)}) collective-permute-start(bf16[144,1280]{1,0:T(8,128)(2,1)S(1)} %fusion.18.refs_4_), channel_id=1, source_target_pairs={{0,4},{2,6},{8,0},{10,2},{16,8},{18,10},{24,16},{26,18},{28,24},{3... | collective-permute-start | bytes 1105928 | tf_op jit(solution)/shard_map/ppermute | solution.py:457
  10.6 10.3 %collective-permute-start.4 = (bf16[144,1280]{1,0:T(8,128)(2,1)S(1)}, bf16[144,1280]{1,0:T(8,128)(2,1)S(1)}, u32[]{:S(2)}, u32[]{:S(2)}) collective-permute-start(bf16[144,1280]{1,0:T(8,128)(2,1)S(1)} %fusion.18.refs_4_), channel_id=1, source_target_pairs={{0,8},{2,10},{8,16},{10,18},{16,24},{18,26},{24,28},{26,30},{28,20... | collective-permute-start | bytes 1105928 | tf_op jit(solution)/shard_map/ppermute | solution.py:456
  54.3 14.3 %collective-permute-start.15 = (bf16[1024,512]{1,0:T(8,128)(2,1)S(1)}, bf16[1024,512]{1,0:T(8,128)(2,1)S(1)}, u32[]{:S(2)}, u32[]{:S(2)}) collective-permute-start(bf16[1024,512]{1,0:T(8,128)(2,1)S(1)} %get-tuple-element.100.mine), channel_id=1, source_target_pairs={{0,2},{2,0},{4,6},{6,4},{8,10},{10,8},{12,14},{14,12},{16,18},{18,... | collective-permute-start | bytes 3145736 | tf_op jit(solution)/shard_map/ppermute | solution.py:444
  56.5 10.1 %collective-permute-start.19 = (bf16[128,1024]{1,0:T(8,128)(2,1)S(1)}, bf16[128,1024]{1,0:T(8,128)(2,1)S(1)}, u32[]{:S(2)}, u32[]{:S(2)}) collective-permute-start(bf16[128,1024]{1,0:T(8,128)(2,1)S(1)} %bitcast.209), channel_id=1, source_target_pairs={{0,4},{2,6},{8,0},{10,2},{16,8},{18,10},{24,16},{26,18},{28,24},{3... | collective-permute-start | bytes 786440 | tf_op jit(solution)/shard_map/ppermute | solution.py:456
  60.3 10.3 %collective-permute-start.28 = (bf16[128,1024]{1,0:T(8,128)(2,1)S(1)}, bf16[128,1024]{1,0:T(8,128)(2,1)S(1)}, u32[]{:S(2)}, u32[]{:S(2)}) collective-permute-start(bf16[128,1024]{1,0:T(8,128)(2,1)S(1)} %dynamic-slice_bitcast_fusion.refs_13_), channel_id=1, source_target_pairs={{0,8},{2,10},{8,16},{10,18},{16,24},{18,26},{24,28},{26,30},{28,20... | collective-permute-start | bytes 786440 | tf_op jit(solution)/shard_map/ppermute | solution.py:457
  66.6 13.3 %collective-permute-start.21 = (bf16[128,1024]{1,0:T(8,128)(2,1)S(1)}, bf16[128,1024]{1,0:T(8,128)(2,1)S(1)}, u32[]{:S(2)}, u32[]{:S(2)}) collective-permute-start(bf16[128,1024]{1,0:T(8,128)(2,1)S(1)} %collective-permute-done.19.refs_5_), channel_id=1, source_target_pairs={{0,4},{2,6},{8,0},{10,2},{16,8},{18,10},{24,16},{26,18},{28,24},{3... | collective-permute-start | bytes 786440 | tf_op jit(solution)/shard_map/ppermute | solution.py:456
  68.2 11.7 %collective-permute-start.22 = (bf16[128,1024]{1,0:T(8,128)(2,1)S(1)}, bf16[128,1024]{1,0:T(8,128)(2,1)S(1)}, u32[]{:S(2)}, u32[]{:S(2)}) collective-permute-start(bf16[128,1024]{1,0:T(8,128)(2,1)S(1)} %collective-permute-done.20.refs_6_), channel_id=1, source_target_pairs={{0,8},{2,10},{8,16},{10,18},{16,24},{18,26},{24,28},{26,30},{28,20... | collective-permute-start | bytes 786440 | tf_op jit(solution)/shard_map/ppermute | solution.py:457
  69.4 10.5 %collective-permute-start.16 = (bf16[128,1024]{1,0:T(8,128)(2,1)S(1)}, bf16[128,1024]{1,0:T(8,128)(2,1)S(1)}, u32[]{:S(2)}, u32[]{:S(2)}) collective-permute-start(bf16[128,1024]{1,0:T(8,128)(2,1)S(1)} %get-tuple-element.103.refs_0_), channel_id=1, source_target_pairs={{0,1},{1,0},{2,3},{3,2},{4,5},{5,4},{6,7},{7,6},{8,9},{9,8},{10,11... | collective-permute-start | bytes 786440 | tf_op jit(solution)/shard_map/ppermute | solution.py:447
  74.3 11.2 %collective-permute-start.29 = (bf16[128,1024]{1,0:T(8,128)(2,1)S(1)}, bf16[128,1024]{1,0:T(8,128)(2,1)S(1)}, u32[]{:S(2)}, u32[]{:S(2)}) collective-permute-start(bf16[128,1024]{1,0:T(8,128)(2,1)S(1)} %collective-permute-done.27.refs_14_), channel_id=1, source_target_pairs={{0,4},{2,6},{8,0},{10,2},{16,8},{18,10},{24,16},{26,18},{28,24},{3... | collective-permute-start | bytes 786440 | tf_op jit(solution)/shard_map/ppermute | solution.py:456
  75.8 9.7 %collective-permute-start.30 = (bf16[128,1024]{1,0:T(8,128)(2,1)S(1)}, bf16[128,1024]{1,0:T(8,128)(2,1)S(1)}, u32[]{:S(2)}, u32[]{:S(2)}) collective-permute-start(bf16[128,1024]{1,0:T(8,128)(2,1)S(1)} %collective-permute-done.28.refs_15_), channel_id=1, source_target_pairs={{0,8},{2,10},{8,16},{10,18},{16,24},{18,26},{24,28},{26,30},{28,20... | collective-permute-start | bytes 786440 | tf_op jit(solution)/shard_map/ppermute | solution.py:457
  79.9 11.2 %collective-permute-start.23 = (bf16[128,1024]{1,0:T(8,128)(2,1)S(1)}, bf16[128,1024]{1,0:T(8,128)(2,1)S(1)}, u32[]{:S(2)}, u32[]{:S(2)}) collective-permute-start(bf16[128,1024]{1,0:T(8,128)(2,1)S(1)} %collective-permute-done.21.refs_7_), channel_id=1, source_target_pairs={{0,4},{2,6},{8,0},{10,2},{16,8},{18,10},{24,16},{26,18},{28,24},{3... | collective-permute-start | bytes 786440 | tf_op jit(solution)/shard_map/ppermute | solution.py:456
  81.5 9.7 %collective-permute-start.24 = (bf16[128,1024]{1,0:T(8,128)(2,1)S(1)}, bf16[128,1024]{1,0:T(8,128)(2,1)S(1)}, u32[]{:S(2)}, u32[]{:S(2)}) collective-permute-start(bf16[128,1024]{1,0:T(8,128)(2,1)S(1)} %collective-permute-done.22.refs_8_), channel_id=1, source_target_pairs={{0,8},{2,10},{8,16},{10,18},{16,24},{18,26},{24,28},{26,30},{28,20... | collective-permute-start | bytes 786440 | tf_op jit(solution)/shard_map/ppermute | solution.py:457
  144.0 11.8 %collective-permute-start.44 = (bf16[1024,512]{1,0:T(8,128)(2,1)}, bf16[1024,512]{1,0:T(8,128)(2,1)}, u32[]{:S(2)}, u32[]{:S(2)}) collective-permute-start(bf16[1024,512]{1,0:T(8,128)(2,1)} %get-tuple-element.137), channel_id=1, source_target_pairs={{0,2},{2,0},{4,6},{6,4},{8,10},{10,8},{12,14},{14,12},{16,18},{18,... | collective-permute-start | bytes 3145736 | tf_op jit(solution)/shard_map/ppermute | solution.py:444
  147.1 21.7 %collective-permute-start.69 = (bf16[128,1024]{1,0:T(8,128)(2,1)S(1)}, bf16[128,1024]{1,0:T(8,128)(2,1)}, u32[]{:S(2)}, u32[]{:S(2)}) collective-permute-start(bf16[128,1024]{1,0:T(8,128)(2,1)S(1)} %pad_maximum_fusion.9), channel_id=1, source_target_pairs={{0,8},{2,10},{8,16},{10,18},{16,24},{18,26},{24,28},{26,30},{28,20... | collective-permute-start | bytes 786440 | tf_op jit(solution)/shard_map/ppermute | solution.py:467
  151.3 17.6 %collective-permute-start.70 = (bf16[128,1024]{1,0:T(8,128)(2,1)}, bf16[128,1024]{1,0:T(8,128)(2,1)}, u32[]{:S(2)}, u32[]{:S(2)}) collective-permute-start(bf16[128,1024]{1,0:T(8,128)(2,1)} %pad_maximum_fusion.10), channel_id=1, source_target_pairs={{0,4},{2,6},{8,0},{10,2},{16,8},{18,10},{24,16},{26,18},{28,24},{3... | collective-permute-start | bytes 786440 | tf_op jit(solution)/shard_map/ppermute | solution.py:468
  153.8 15.0 %collective-permute-start.62 = (bf16[128,1024]{1,0:T(8,128)(2,1)}, bf16[128,1024]{1,0:T(8,128)(2,1)}, u32[]{:S(2)}, u32[]{:S(2)}) collective-permute-start(bf16[128,1024]{1,0:T(8,128)(2,1)} %get-tuple-element.195), channel_id=1, source_target_pairs={{0,4},{2,6},{8,0},{10,2},{16,8},{18,10},{24,16},{26,18},{28,24},{3... | collective-permute-start | bytes 786440 | tf_op jit(solution)/shard_map/ppermute | solution.py:468
  155.4 13.4 %collective-permute-start.61 = (bf16[128,1024]{1,0:T(8,128)(2,1)}, bf16[128,1024]{1,0:T(8,128)(2,1)}, u32[]{:S(2)}, u32[]{:S(2)}) collective-permute-start(bf16[128,1024]{1,0:T(8,128)(2,1)} %get-tuple-element.196), channel_id=1, source_target_pairs={{0,8},{2,10},{8,16},{10,18},{16,24},{18,26},{24,28},{26,30},{28,20... | collective-permute-start | bytes 786440 | tf_op jit(solution)/shard_map/ppermute | solution.py:467
  170.3 16.8 %collective-permute-start.63 = (bf16[128,1024]{1,0:T(8,128)(2,1)S(1)}, bf16[128,1024]{1,0:T(8,128)(2,1)S(1)}, u32[]{:S(2)}, u32[]{:S(2)}) collective-permute-start(bf16[128,1024]{1,0:T(8,128)(2,1)S(1)} %get-tuple-element.193), channel_id=1, source_target_pairs={{0,8},{2,10},{8,16},{10,18},{16,24},{18,26},{24,28},{26,30},{28,20... | collective-permute-start | bytes 786440 | tf_op jit(solution)/shard_map/ppermute | solution.py:479
  172.3 16.4 %collective-permute-start.64 = (bf16[128,1024]{1,0:T(8,128)(2,1)S(1)}, bf16[128,1024]{1,0:T(8,128)(2,1)S(1)}, u32[]{:S(2)}, u32[]{:S(2)}) collective-permute-start(bf16[128,1024]{1,0:T(8,128)(2,1)S(1)} %get-tuple-element.194), channel_id=1, source_target_pairs={{0,4},{2,6},{8,0},{10,2},{16,8},{18,10},{24,16},{26,18},{28,24},{3... | collective-permute-start | bytes 786440 | tf_op jit(solution)/shard_map/ppermute | solution.py:480
  176.8 13.6 %collective-permute-start.45 = (bf16[2,128,1024]{2,1,0:T(8,128)(2,1)S(1)}, bf16[2,128,1024]{2,1,0:T(8,128)(2,1)S(1)}, u32[]{:S(2)}, u32[]{:S(2)}) collective-permute-start(bf16[2,128,1024]{2,1,0:T(8,128)(2,1)S(1)} %get-tuple-element.144), channel_id=1, source_target_pairs={{0,2},{2,0},{4,6},{6,4},{8,10},{10,8},{12,14},{14,12},{16,18},{18,... | collective-permute-start | bytes 1572872 | tf_op jit(solution)/shard_map/ppermute | solution.py:444
  187.2 11.4 %collective-permute-start.72 = (bf16[128,1024]{1,0:T(8,128)(2,1)S(1)}, bf16[128,1024]{1,0:T(8,128)(2,1)S(1)}, u32[]{:S(2)}, u32[]{:S(2)}) collective-permute-start(bf16[128,1024]{1,0:T(8,128)(2,1)S(1)} %get-tuple-element.183), channel_id=1, source_target_pairs={{0,8},{2,10},{8,16},{10,18},{16,24},{18,26},{24,28},{26,30},{28,20... | collective-permute-start | bytes 786440 | tf_op jit(solution)/shard_map/ppermute | solution.py:479
  188.7 9.8 %collective-permute-start.74 = (bf16[128,1024]{1,0:T(8,128)(2,1)S(1)}, bf16[128,1024]{1,0:T(8,128)(2,1)S(1)}, u32[]{:S(2)}, u32[]{:S(2)}) collective-permute-start(bf16[128,1024]{1,0:T(8,128)(2,1)S(1)} %get-tuple-element.184), channel_id=1, source_target_pairs={{0,4},{2,6},{8,0},{10,2},{16,8},{18,10},{24,16},{26,18},{28,24},{3... | collective-permute-start | bytes 786440 | tf_op jit(solution)/shard_map/ppermute | solution.py:480
  205.1 20.6 %collective-permute-start.66 = (bf16[128,1024]{1,0:T(8,128)(2,1)S(1)}, bf16[128,1024]{1,0:T(8,128)(2,1)}, u32[]{:S(2)}, u32[]{:S(2)}) collective-permute-start(bf16[128,1024]{1,0:T(8,128)(2,1)S(1)} %pad_maximum_fusion.8), channel_id=1, source_target_pairs={{0,1},{1,0},{2,3},{3,2},{4,5},{5,4},{6,7},{7,6},{8,9},{9,8},{10,11... | collective-permute-start | bytes 786440 | tf_op jit(solution)/shard_map/ppermute | solution.py:447
  224.1 10.9 %collective-permute-start.56 = (bf16[144,1280]{1,0:T(8,128)(2,1)}, bf16[144,1280]{1,0:T(8,128)(2,1)S(1)}, u32[]{:S(2)}, u32[]{:S(2)}) collective-permute-start(bf16[144,1280]{1,0:T(8,128)(2,1)} %pad_maximum_fusion.3), channel_id=1, source_target_pairs={{0,1},{1,0},{2,3},{3,2},{4,5},{5,4},{6,7},{7,6},{8,9},{9,8},{10,11... | collective-permute-start | bytes 1105928 | tf_op jit(solution)/shard_map/ppermute | solution.py:447
  (70 other events, 595.0 us)
